TPU v7x, 256 devices: a whole 4x4x8 slice. The times are simulated.
256 devices in a mesh: rows: 32 (over z, x), cols: 8 (over y, core).
Axes of the slice: x: 4, y: 4, z: 8, core: 2. Of those that a mesh axis runs over, the one named last changes fastest.
Arguments:
- features: bfloat16 [256, 256, 512], P('rows', 'cols'), may hold values from -6 to 6
- kernel: bfloat16 [4608, 512], replicated, may hold values from -0.09375 to 0.09375
- out_grad: bfloat16 [256, 256, 512], P('rows', 'cols'), may hold values from -6 to 6
- projector: bfloat16 [4096, 2048], P('rows', 'cols'), may hold values from -0.375 to 0.375
- mixers: bfloat16 [2, 128, 256], replicated, may hold values from -0.5 to 0.5
Outputs:
- output: bfloat16 [256, 256, 512], P('rows', 'cols')
- grad_features: bfloat16 [256, 256, 512], P('rows', 'cols')
- grad_kernel: float32 [9, 512, 512], P(None, 'rows', 'cols')
- sketch: bfloat16 [128, 4608], P('cols', 'rows')
All inputs are finite; a program needn't handle non-finite values.
Results may differ from a plain program's by a relative error of at most 0.015.
Values may be sent and summed in bfloat16 or wider, within the bound.
A program may use at most 192 MiB of HBM per device.

v0:
```python
import jax
import jax.numpy as jnp
from jax import lax
from jax.sharding import PartitionSpec as P

NS_STEPS = 5


def padded_2(x, sides, width):
    for axis, dim in sides:
        size, length = (lax.axis_size(axis), x.shape[dim])
        up = [(i, (i + 1) % size) for i in range(size - 1)]
        down = [(j, i) for i, j in up]
        last = lax.slice_in_dim(x, length - width, length, axis=dim)
        first = lax.slice_in_dim(x, 0, width, axis=dim)
        before = lax.ppermute(last, axis, up)
        after = lax.ppermute(first, axis, down)
        x = jnp.concatenate([before, x, after], axis=dim)
    return x


def swapped(x, axis, apart):
    return lax.ppermute(x, axis, [(i, i ^ 1 << apart) for i in range(lax.axis_size(axis))])


def finish_merge(gram_matrix, stacked, mix_matrix):
    size_two = gram_matrix.shape[0]
    identity = jnp.eye(size_two, dtype=jnp.float32)
    spread = gram_matrix / (jnp.trace(gram_matrix) + 1e-06) - identity / size_two
    spread = spread / (jnp.sqrt(jnp.sum(spread * spread)) + 1e-06)
    for sweep in range(NS_STEPS):
        square = jnp.dot(spread, spread, precision=lax.Precision.HIGHEST)
        spread = 1.5 * spread - 0.5 * jnp.dot(spread, square, precision=lax.Precision.HIGHEST)
    keeper = 0.5 * (identity + spread)
    combiner = jnp.dot(
        mix_matrix.astype(jnp.float32), keeper, precision=lax.Precision.HIGHEST
    ).astype(jnp.bfloat16)
    return jnp.dot(combiner, stacked, preferred_element_type=jnp.float32).astype(jnp.bfloat16)


def shrink_merge(upper_part, lower_part, mix_matrix):
    contract = (((1,), (1,)), ((), ()))
    upper_upper = lax.dot_general(
        upper_part, upper_part, contract, preferred_element_type=jnp.float32
    )
    upper_lower = lax.dot_general(
        upper_part, lower_part, contract, preferred_element_type=jnp.float32
    )
    lower_lower = lax.dot_general(
        lower_part, lower_part, contract, preferred_element_type=jnp.float32
    )
    gram_matrix = jnp.concatenate(
        [
            jnp.concatenate([upper_upper, upper_lower], axis=1),
            jnp.concatenate([upper_lower.T, lower_lower], axis=1),
        ],
        axis=0,
    )
    stacked = jnp.concatenate([upper_part, lower_part], axis=0)
    return finish_merge(gram_matrix, stacked, mix_matrix)


def tap_stack(padded, band_rows, band_cols, flipped):
    pieces = []
    for row_tap in range(3):
        for col_tap in range(3):
            row_start = 2 - row_tap if flipped else row_tap
            col_start = 2 - col_tap if flipped else col_tap
            pieces.append(
                padded[row_start : row_start + band_rows, col_start : col_start + band_cols, :]
            )
    return jnp.concatenate(pieces, axis=2)


def body(features, kernel, out_grad, projector, mixers):
    band_rows, band_cols, channels = features.shape
    pixels = band_rows * band_cols
    padded = padded_2(features, (("rows", 0), ("cols", 1)), 1)
    patches = tap_stack(padded, band_rows, band_cols, False).reshape(pixels, 9 * channels)
    output = jnp.dot(patches, kernel, preferred_element_type=jnp.float32)
    output = output.astype(jnp.bfloat16).reshape(band_rows, band_cols, channels)
    grad_padded = padded_2(out_grad, (("rows", 0), ("cols", 1)), 1)
    grad_patches = tap_stack(grad_padded, band_rows, band_cols, True).reshape(pixels, 9, channels)
    grad_features = lax.dot_general(
        grad_patches,
        kernel.reshape(9, channels, channels),
        (((1, 2), (0, 2)), ((), ())),
        preferred_element_type=jnp.float32,
    )
    grad_features = grad_features.astype(jnp.bfloat16).reshape(band_rows, band_cols, channels)
    row_count = lax.axis_size("rows")
    col_count = lax.axis_size("cols")
    split_patches = patches.reshape(pixels, 9, row_count, channels // row_count)
    split_grad = out_grad.reshape(pixels, col_count, channels // col_count)
    weight_terms = jnp.einsum(
        "pkri,pco->rckio", split_patches, split_grad, preferred_element_type=jnp.float32
    )
    flat_terms = weight_terms.reshape((row_count * col_count,) + weight_terms.shape[2:])
    summed = lax.psum_scatter(flat_terms, ("rows", "cols"), scatter_dimension=0, tiled=True)
    grad_kernel = summed.reshape(9, channels // row_count, channels // col_count)
    sketch = jnp.dot(projector, patches, preferred_element_type=jnp.float32).astype(jnp.bfloat16)
    row_index = lax.axis_index("rows")
    col_index = lax.axis_index("cols")
    for tree_level in range(row_count.bit_length() - 1):
        partner = swapped(sketch, "rows", tree_level)
        is_lower = row_index >> tree_level & 1 == 0
        sketch = shrink_merge(
            jnp.where(is_lower, sketch, partner), jnp.where(is_lower, partner, sketch), mixers[0]
        )
    for tree_level in range(col_count.bit_length() - 1):
        partner = swapped(sketch, "cols", tree_level)
        is_lower = col_index >> tree_level & 1 == 0
        sketch = shrink_merge(
            jnp.where(is_lower, sketch, partner), jnp.where(is_lower, partner, sketch), mixers[1]
        )
    rank_share = sketch.shape[0] // col_count
    patch_share = sketch.shape[1] // row_count
    own_block = lax.dynamic_slice(
        sketch, (col_index * rank_share, row_index * patch_share), (rank_share, patch_share)
    )
    return (output, grad_features, grad_kernel, own_block)


def solution(mesh):
    in_specs = (P("rows", "cols", None), P(), P("rows", "cols", None), P("rows", "cols"), P())
    out_specs = (
        P("rows", "cols", None),
        P("rows", "cols", None),
        P(None, "rows", "cols"),
        P("cols", "rows"),
    )
    return jax.shard_map(body, mesh=mesh, in_specs=in_specs, out_specs=out_specs, check_vma=False)
```

profile of v0, /device:TPU:8, one launch (start us, length us, event | category | flops | bytes accessed | tf_op | source)
XLA Modules:
  0.0 777.0 jit_solution(6794121425388190363)
XLA Ops:
  7.2 0.8 fusion.152
  8.1 3.4 collective-permute-start
  11.5 1.3 collective-permute-start.1
  13.0 1.0 constant_dynamic-update-slice_fusion.1
  14.0 3.3 collective-permute-done.1
  17.3 1.9 collective-permute-start.2
  19.2 3.6 collective-permute-start.3
  23.0 1.3 collective-permute-done.3
  25.4 0.9 copy-done.2
  26.3 1.5 collective-permute-start.8
  27.8 26.8 %collective-permute-done.8 = bf16[128,4608]{1,0:T(8,128)(2,1)} collective-permute-done((bf16[128,4608]{1,0:T(8,128)(2,1)S(1)}, bf16[128,4608]{1,0:T(8,128)(2,1)}, u32[]{:S(2)}, u32[]{:S(2)}) %collective-permute-start.8) | collective-permute-done | bytes 1179680 | tf_op jit(solution)/shard_map/ppermute | solution.py:23
  54.6 1.8 broadcast_select_fusion.1
  59.2 0.7 multiply_reduce_fusion.7
  66.9 1.5 convolution_convert_fusion.7
  68.4 4.8 collective-permute-start.9
  73.2 27.0 %collective-permute-done.9 = bf16[128,4608]{1,0:T(8,128)(2,1)} collective-permute-done((bf16[128,4608]{1,0:T(8,128)(2,1)}, bf16[128,4608]{1,0:T(8,128)(2,1)}, u32[]{:S(2)}, u32[]{:S(2)}) %collective-permute-start.9) | collective-permute-done | bytes 1179680 | tf_op jit(solution)/shard_map/ppermute | solution.py:23
  100.2 1.8 broadcast_select_fusion.3
  104.8 0.7 multiply_reduce_fusion.6
  112.5 1.5 convolution_convert_fusion.6
  114.0 2.0 collective-permute-start.10
  116.1 26.6 %collective-permute-done.10 = bf16[128,4608]{1,0:T(8,128)(2,1)} collective-permute-done((bf16[128,4608]{1,0:T(8,128)(2,1)}, bf16[128,4608]{1,0:T(8,128)(2,1)}, u32[]{:S(2)}, u32[]{:S(2)}) %collective-permute-start.10) | collective-permute-done | bytes 1179680 | tf_op jit(solution)/shard_map/ppermute | solution.py:23
  142.7 1.8 broadcast_select_fusion.5
  155.0 1.5 convolution_convert_fusion.5
  156.5 5.9 collective-permute-start.11
  162.4 51.3 %collective-permute-done.11 = bf16[128,4608]{1,0:T(8,128)(2,1)} collective-permute-done((bf16[128,4608]{1,0:T(8,128)(2,1)}, bf16[128,4608]{1,0:T(8,128)(2,1)}, u32[]{:S(2)}, u32[]{:S(2)}) %collective-permute-start.11) | collective-permute-done | bytes 1179680 | tf_op jit(solution)/shard_map/ppermute | solution.py:23
  213.7 1.8 broadcast_select_fusion.7
  226.0 1.5 convolution_convert_fusion.4
  227.5 3.5 collective-permute-start.12
  231.1 53.4 %collective-permute-done.12 = bf16[128,4608]{1,0:T(8,128)(2,1)} collective-permute-done((bf16[128,4608]{1,0:T(8,128)(2,1)}, bf16[128,4608]{1,0:T(8,128)(2,1)}, u32[]{:S(2)}, u32[]{:S(2)}) %collective-permute-start.12) | collective-permute-done | bytes 1179680 | tf_op jit(solution)/shard_map/ppermute | solution.py:23
  284.5 1.8 broadcast_select_fusion.9
  289.0 0.7 multiply_reduce_fusion.3
  296.8 1.5 convolution_convert_fusion.3
  298.9 2.7 collective-permute-start.4
  301.7 1.5 collective-permute-start.5
  303.5 10.3 %copy.53 = bf16[8,32,4608]{1,0,2:T(8,128)(2,1)} copy(bf16[8,32,4608]{2,1,0:T(8,128)(2,1)} %copy-done.2) | data formatting | bytes 4718592 | tf_op jit(solution)/shard_map/concatenate | solution.py:72
  313.9 11.0 %reshape.41 = bf16[256,9,32,16,1]{0,3,2,1,4:T(8,128)(2,1)S(1)} reshape(bf16[8,32,4608]{1,0,2:T(8,128)(2,1)} %copy.53) | data formatting | bytes 4718592 | tf_op jit(solution)/shard_map/reshape;reshape | solution.py:93
  324.9 2.6 fusion.26
  327.5 6.8 copy.55
  334.3 1.8 broadcast_select_fusion.11
  346.7 1.5 convolution_convert_fusion.2
  348.4 0.8 constant_dynamic-update-slice_fusion.4
  349.2 3.5 collective-permute-start.6
  352.7 1.9 collective-permute-start.7
  354.6 20.1 %collective-permute-done.6 = bf16[10,1,512]{2,1,0:T(2,128)(2,1)S(1)} collective-permute-done((bf16[10,1,512]{2,1,0:T(2,128)(2,1)S(1)}, bf16[10,1,512]{2,1,0:T(2,128)(2,1)S(1)}, u32[]{:S(2)}, u32[]{:S(2)}) %collective-permute-start.6) | collective-permute-done | bytes 10272 | tf_op jit(solution)/shard_map/ppermute | solution.py:17
  374.7 0.9 fusion.100
  375.6 1.5 fusion.112
  377.1 0.8 fusion.96
  378.0 0.8 fusion.98
  378.8 0.8 constant_dynamic-update-slice_fusion.7
  379.6 0.8 fusion.94
  380.4 0.8 fusion.111
  381.2 1.8 broadcast_select_fusion.13
  393.6 1.5 convolution_convert_fusion.1
  395.1 2.4 collective-permute-start.15
  397.5 0.7 fusion.110
  398.3 0.8 fusion.109
  399.1 5.7 reshape.34
  404.7 4.6 convolution_convert_fusion.8
  409.4 6.0 fusion.33
  415.4 4.6 collective-permute-done.15
  420.0 1.8 broadcast_select_fusion.15
  424.6 0.7 multiply_reduce_fusion
  432.9 0.7 dynamic_slice.6
  433.6 336.2 %reduce-scatter.2.cloned.1.call-done = f32[1,9,16,64]{3,2,1,0:T(8,128)} async-done(((f32[256,9,16,64]{3,2,1,0:T(8,128)}), f32[1,9,16,64]{3,2,1,0:T(8,128)}) %reduce-scatter.2.cloned.1.call-update) | async-done | bytes 36880 | tf_op jit(solution)/shard_map/reduce_scatter | solution.py:99
  (185 shorter events, 73.0 us)
Async XLA Ops:
  7.2 17.7 %copy-start = (bf16[128,256]{1,0:T(8,128)(2,1)S(1)}, bf16[128,256]{1,0:T(8,128)(2,1)}, u32[]{:S(2)}) copy-start(bf16[128,256]{1,0:T(8,128)(2,1)} %param.8) | copy-start | bytes 196612
  7.2 15.8 %copy-start.5 = (bf16[8,32,512]{2,1,0:T(8,128)(2,1)S(1)}, bf16[8,32,512]{2,1,0:T(8,128)(2,1)}, u32[]{:S(2)}) copy-start(bf16[8,32,512]{2,1,0:T(8,128)(2,1)} %param.5) | copy-start | bytes 786436
  7.2 762.6 %reduce-scatter.2.cloned.1.call-start = ((), (), s32[]{:S(2)}) async-start(), calls=%async_computation.1 | async-start | bytes 18948096 | tf_op jit(solution)/shard_map/reduce_scatter | solution.py:99
  8.1 5.0 collective-permute-start
  11.5 5.8 collective-permute-start.1
  17.3 5.6 collective-permute-start.2
  19.2 5.1 collective-permute-start.3
  24.9 1.4 copy-start.2
  26.3 1.5 copy-start.6
  26.3 28.3 %collective-permute-start.8 = (bf16[128,4608]{1,0:T(8,128)(2,1)S(1)}, bf16[128,4608]{1,0:T(8,128)(2,1)}, u32[]{:S(2)}, u32[]{:S(2)}) collective-permute-start(bf16[128,4608]{1,0:T(8,128)(2,1)S(1)} %fusion), channel_id=1, source_target_pairs={{0,8},{8,0},{16,24},{24,16},{32,40},{40,32},{48,56},{56,48},{64,72... | collective-permute-start | bytes 3538952 | tf_op jit(solution)/shard_map/ppermute | solution.py:23
  64.8 1.8 copy-start.8
  68.4 31.8 %collective-permute-start.9 = (bf16[128,4608]{1,0:T(8,128)(2,1)}, bf16[128,4608]{1,0:T(8,128)(2,1)}, u32[]{:S(2)}, u32[]{:S(2)}) collective-permute-start(bf16[128,4608]{1,0:T(8,128)(2,1)} %convolution_convert_fusion.7), channel_id=1, source_target_pairs={{0,16},{8,24},{16,0},{24,8},{32,48},{40,56},{48,32},{56,40},{64,80... | collective-permute-start | bytes 3538952 | tf_op jit(solution)/shard_map/ppermute | solution.py:23
  114.0 28.6 %collective-permute-start.10 = (bf16[128,4608]{1,0:T(8,128)(2,1)}, bf16[128,4608]{1,0:T(8,128)(2,1)}, u32[]{:S(2)}, u32[]{:S(2)}) collective-permute-start(bf16[128,4608]{1,0:T(8,128)(2,1)} %convolution_convert_fusion.6), channel_id=1, source_target_pairs={{0,32},{8,40},{16,48},{24,56},{32,0},{40,8},{48,16},{56,24},{64,96... | collective-permute-start | bytes 3538952 | tf_op jit(solution)/shard_map/ppermute | solution.py:23
  156.5 57.2 %collective-permute-start.11 = (bf16[128,4608]{1,0:T(8,128)(2,1)}, bf16[128,4608]{1,0:T(8,128)(2,1)}, u32[]{:S(2)}, u32[]{:S(2)}) collective-permute-start(bf16[128,4608]{1,0:T(8,128)(2,1)} %convolution_convert_fusion.5), channel_id=1, source_target_pairs={{0,64},{8,72},{16,80},{24,88},{32,96},{40,104},{48,112},{56,120},{... | collective-permute-start | bytes 3538952 | tf_op jit(solution)/shard_map/ppermute | solution.py:23
  227.5 56.9 %collective-permute-start.12 = (bf16[128,4608]{1,0:T(8,128)(2,1)}, bf16[128,4608]{1,0:T(8,128)(2,1)}, u32[]{:S(2)}, u32[]{:S(2)}) collective-permute-start(bf16[128,4608]{1,0:T(8,128)(2,1)} %convolution_convert_fusion.4), channel_id=1, source_target_pairs={{0,128},{8,136},{16,144},{24,152},{32,160},{40,168},{48,176},{56,1... | collective-permute-start | bytes 3538952 | tf_op jit(solution)/shard_map/ppermute | solution.py:23
  296.8 1.6 copy-start.4
  298.3 36.0 %collective-permute-start.13 = (bf16[128,4608]{1,0:T(8,128)(2,1)}, bf16[128,4608]{1,0:T(8,128)(2,1)}, u32[]{:S(2)}, u32[]{:S(2)}) collective-permute-start(bf16[128,4608]{1,0:T(8,128)(2,1)} %convolution_convert_fusion.3), channel_id=1, source_target_pairs={{0,1},{1,0},{2,3},{3,2},{4,5},{5,4},{6,7},{7,6},{8,9},{9,8},{10,11... | collective-permute-start | bytes 3538952 | tf_op jit(solution)/shard_map/ppermute | solution.py:23
  298.9 4.5 collective-permute-start.4
  301.7 46.7 %collective-permute-start.5 = (bf16[1,32,512]{2,1,0:T(8,128)(2,1)}, bf16[1,32,512]{2,1,0:T(8,128)(2,1)}, u32[]{:S(2)}, u32[]{:S(2)}) collective-permute-start(bf16[1,32,512]{2,1,0:T(8,128)(2,1)} %get-tuple-element.24), channel_id=1, source_target_pairs={{8,0},{16,8},{24,16},{32,24},{40,32},{48,40},{56,48},{64,56},{72,6... | collective-permute-start | bytes 98312 | tf_op jit(solution)/shard_map/ppermute | solution.py:17
  303.5 10.4 %copy-start.10 = (bf16[1,32,512]{2,1,0:T(8,128)(2,1)}, bf16[1,32,512]{2,1,0:T(8,128)(2,1)S(1)}, u32[]{:S(2)}) copy-start(bf16[1,32,512]{2,1,0:T(8,128)(2,1)S(1)} %collective-permute-done.4) | copy-start | bytes 98308
  344.5 1.8 copy-start.9
  348.2 33.0 %collective-permute-start.14 = (bf16[128,4608]{1,0:T(8,128)(2,1)}, bf16[128,4608]{1,0:T(8,128)(2,1)}, u32[]{:S(2)}, u32[]{:S(2)}) collective-permute-start(bf16[128,4608]{1,0:T(8,128)(2,1)} %convolution_convert_fusion.2), channel_id=1, source_target_pairs={{0,2},{1,3},{2,0},{3,1},{4,6},{5,7},{6,4},{7,5},{8,10},{9,11},{10,... | collective-permute-start | bytes 3538952 | tf_op jit(solution)/shard_map/ppermute | solution.py:23
  349.2 25.5 %collective-permute-start.6 = (bf16[10,1,512]{2,1,0:T(2,128)(2,1)S(1)}, bf16[10,1,512]{2,1,0:T(2,128)(2,1)S(1)}, u32[]{:S(2)}, u32[]{:S(2)}) collective-permute-start(bf16[10,1,512]{2,1,0:T(2,128)(2,1)S(1)} %get-tuple-element.21), channel_id=1, source_target_pairs={{1,0},{2,1},{3,2},{4,3},{5,4},{6,5},{7,6},{9,8},{10,9},{11,10},{12... | collective-permute-start | bytes 30728 | tf_op jit(solution)/shard_map/ppermute | solution.py:17
  352.7 24.4 %collective-permute-start.7 = (bf16[10,1,512]{2,1,0:T(2,128)(2,1)S(1)}, bf16[10,1,512]{2,1,0:T(2,128)(2,1)S(1)}, u32[]{:S(2)}, u32[]{:S(2)}) collective-permute-start(bf16[10,1,512]{2,1,0:T(2,128)(2,1)S(1)} %get-tuple-element.20), channel_id=1, source_target_pairs={{0,1},{1,2},{2,3},{3,4},{4,5},{5,6},{6,7},{8,9},{9,10},{10,11},{11... | collective-permute-start | bytes 30728 | tf_op jit(solution)/shard_map/ppermute | solution.py:16
  393.6 3.9 copy-start.11
  395.1 24.9 %collective-permute-start.15 = (bf16[128,4608]{1,0:T(8,128)(2,1)}, bf16[128,4608]{1,0:T(8,128)(2,1)}, u32[]{:S(2)}, u32[]{:S(2)}) collective-permute-start(bf16[128,4608]{1,0:T(8,128)(2,1)} %convolution_convert_fusion.1), channel_id=1, source_target_pairs={{0,4},{1,5},{2,6},{3,7},{4,0},{5,1},{6,2},{7,3},{8,12},{9,13},{10,... | collective-permute-start | bytes 3538952 | tf_op jit(solution)/shard_map/ppermute | solution.py:23
  399.1 5.7 copy-start.3
  404.7 4.6 copy-start.7
  432.1 337.7 %copy-start.1 = (bf16[128,256]{1,0:T(8,128)(2,1)S(1)}, bf16[128,256]{1,0:T(8,128)(2,1)}, u32[]{:S(2)}) copy-start(bf16[128,256]{1,0:T(8,128)(2,1)} %param.8) | copy-start | bytes 196612
Sparse Core Ops, SparseCore 0:
  334.4 435.2 reduce-scatter.1
where the time goes:
time: 786 us; the launch traced here: 777 us
  waiting for transfers between devices  551 us (70%)
  matrix products  86.2 us (11%)
  local copies, waits for them, and re-layouts  40.5 us (5%)
  starting transfers between devices  40.2 us (5%)
  other arithmetic  32.6 us (4%)
  between operations  26.5 us (3%)
    reduce_scatter x1, waiting for transfers between devices, body(): lax.psum_scatter(flat_terms, ('rows', 'cols'), scatter_dimension=0, tiled...  336 us
    ppermute x8, waiting for transfers between devices, swapped(): lax.ppermute(x, axis, [(i, i ^ 1 << apart) for i in range(lax.axis_size(a...  190 us
    ppermute x4, waiting for transfers between devices, padded_2(): after = lax.ppermute(first, axis, down)  24.7 us
    dot_general x40, matrix products, finish_merge(): jnp.dot(spread, square, precision=lax.Precision.HIGHEST)  24.1 us
    dot_general x40, matrix products, finish_merge(): square = jnp.dot(spread, spread, precision=lax.Precision.HIGHEST)  23.8 us
    ppermute x8, starting transfers between devices, swapped(): lax.ppermute(x, axis, [(i, i ^ 1 << apart) for i in range(lax.axis_size(a...  20.4 us
  transfers between devices with their start and end apart: 17, of which 11 were waited for; matrix products, arithmetic and copies ran while one was open for 12% of the time, Pallas kernels for 0%

commit v1 on v0

v1 whole, which is shorter than its diff:
```python
import jax
import jax.numpy as jnp
from jax import lax
from jax.experimental import pallas as pl
from jax.experimental.pallas import tpu as pltpu
from jax.sharding import PartitionSpec as P

NS_STEPS = 5
NX, NZ, NY, NC = 4, 8, 4, 2
LANES = 128
CH = 512
RANK = 128
TAPS = 9
QUART = 1152
MESH = pl.DeviceIdType.MESH
F32 = jnp.float32
BF16 = jnp.bfloat16


def dot(a, b):
    return jnp.dot(a, b, preferred_element_type=F32)


def dot_t(a, b):
    return lax.dot_general(a, b, (((1,), (1,)), ((), ())), preferred_element_type=F32)


def split(v):
    high = v.astype(BF16)
    return high, (v - high.astype(F32)).astype(BF16)


def local_kernel(xs, gs, ogt, kern, out, gfeat, wt, acc_o, acc_g, xsp):
    t = pl.program_id(0)

    @pl.when(t == 0)
    def _():
        acc_o[...] = jnp.zeros_like(acc_o)
        acc_g[...] = jnp.zeros_like(acc_g)
        ci = lax.broadcasted_iota(jnp.int32, (CH, CH), 0)
        to = lax.broadcasted_iota(jnp.int32, (CH, CH), 1)
        source = lax.rem(lax.div(to, 16), NZ) * 64 + lax.div(to, 128) * 16 + lax.rem(to, 16)
        perm = jnp.where(ci == source, 1.0, 0.0).astype(BF16)
        for b in range(3):
            xsp[b] = dot(xs[b], perm).astype(BF16)

    a = lax.div(t, 3)
    b = lax.rem(t, 3)
    start = pl.multiple_of(a * 32, 32)
    back = pl.multiple_of((2 - a) * 32, 32)
    weights = kern[0]
    acc_o[...] += dot(xs[b, pl.ds(start, 256), :], weights)
    acc_g[...] += dot_t(gs[2 - b, pl.ds(back, 256), :], weights)
    terms = dot(ogt[...], xsp[b, pl.ds(start, 256), :]).astype(BF16)
    for y in range(NY):
        for core in range(NC):
            for x in range(NX):
                at = (y * NC + core) * 64
                wt[y, core, x, 0] = terms[at : at + 64, x * LANES : (x + 1) * LANES]

    @pl.when(t == TAPS - 1)
    def _():
        out[...] = acc_o[...].astype(BF16)
        gfeat[...] = acc_g[...].astype(BF16)


def local_call(xs, gs, ogt, kernel):
    whole = lambda *shape: pl.BlockSpec(shape, lambda t: (0,) * len(shape))
    return pl.pallas_call(
        local_kernel,
        grid=(TAPS,),
        in_specs=[
            whole(3, 320, CH),
            whole(3, 320, CH),
            whole(CH, 256),
            pl.BlockSpec((1, CH, CH), lambda t: (t, 0, 0)),
        ],
        out_specs=[
            whole(256, CH),
            whole(256, CH),
            pl.BlockSpec((NY, NC, NX, 1, 64, LANES), lambda t: (0, 0, 0, t, 0, 0)),
        ],
        out_shape=[
            jax.ShapeDtypeStruct((256, CH), BF16),
            jax.ShapeDtypeStruct((256, CH), BF16),
            jax.ShapeDtypeStruct((NY, NC, NX, TAPS, 64, LANES), BF16),
        ],
        scratch_shapes=[
            pltpu.VMEM((256, CH), F32),
            pltpu.VMEM((256, CH), F32),
            pltpu.VMEM((3, 320, CH), BF16),
        ],
        compiler_params=pltpu.CompilerParams(vmem_limit_bytes=32 << 20),
        cost_estimate=pl.CostEstimate(
            flops=3 * 2 * 256 * 4608 * 512, bytes_accessed=11 << 20, transcendentals=0
        ),
        name="conv_terms",
    )(xs, gs, ogt, kernel)


def start_spread(gram):
    size = gram.shape[0]
    i = lax.broadcasted_iota(jnp.int32, (size, size), 0)
    j = lax.broadcasted_iota(jnp.int32, (size, size), 1)
    eye = jnp.where(i == j, 1.0, 0.0)
    trace = jnp.sum(gram * eye, keepdims=True)
    spread = gram / (trace + 1e-06) - eye * (1.0 / size)
    return spread / (jnp.sqrt(jnp.sum(spread * spread, keepdims=True)) + 1e-06)


def combiners(grams, mix):
    spreads = [start_spread(gram) for gram in grams]
    for sweep in range(NS_STEPS - 1):
        rounded = [s.astype(BF16) for s in spreads]
        squares = [dot(r, r).astype(BF16) for r in rounded]
        spreads = [
            1.5 * s - 0.5 * dot(r, q) for s, r, q in zip(spreads, rounded, squares)
        ]
    parts = [split(s) for s in spreads]
    squares = [dot(high, high).astype(BF16) for high, low in parts]
    mixed = [dot(mix, high) + dot(mix, low) for high, low in parts]
    wide = mix.astype(F32)
    return [
        (0.5 * wide + 0.75 * m - 0.25 * dot(m.astype(BF16), q)).astype(BF16)
        for m, q in zip(mixed, squares)
    ]


def carried_gram(combiner, gram):
    high, low = split(gram)
    first = dot(combiner, high) + dot(combiner, low)
    high, low = split(first)
    return dot_t(high, combiner) + dot_t(low, combiner)


def tree_kernel(
    wt, bands, proj, mixers, gk, sketch,
    ro, rc, ry, w2, rx, wz, rz, m0, m1, ma, mb, da, db, po, pr, fr, gm, lsem, ssem, rsem,
):
    row, col = lax.axis_index("rows"), lax.axis_index("cols")
    z, x = lax.div(row, NX), lax.rem(row, NX)
    y, core = lax.div(col, NC), lax.rem(col, NC)

    def at(zz, xx, yy, cc):
        return (zz * NX + xx, yy * NC + cc)

    x_peers = [at(z, lax.rem(x + d, NX), y, core) for d in range(1, NX)]
    y_peers = [at(z, x, lax.rem(y + d, NY), core) for d in range(1, NY)]
    z_peers = [at(lax.rem(z + d, NZ), x, y, core) for d in range(1, NZ)]
    core_peer = at(z, x, y, 1 - core)

    barrier = pltpu.get_barrier_semaphore()
    peers = x_peers + y_peers + z_peers + [core_peer]
    for peer in peers:
        pl.semaphore_signal(barrier, inc=1, device_id=peer, device_id_type=MESH)

    started = []

    def send(src, dst, i, peer):
        copy = pltpu.make_async_remote_copy(
            src_ref=src,
            dst_ref=dst,
            send_sem=ssem.at[i],
            recv_sem=rsem.at[i],
            device_id=peer,
            device_id_type=MESH,
        )
        copy.start()
        started.append(copy)
        return copy

    own_terms = pltpu.make_async_copy(wt.at[:, core], ro, lsem.at[0])
    own_terms.start()
    pl.semaphore_wait(barrier, len(peers))
    core_copy = send(wt.at[:, 1 - core], rc, 0, core_peer)

    for j in range(NX):
        slot = lax.rem(j - x + NX, NX)
        p = proj[slot]
        for t in range(TAPS):
            a, b = t // 3, t % 3
            part = dot(p, bands[b, slot, a * 32 : a * 32 + 256, :]).astype(BF16)
            for i in range(4):
                q, lane = (4 * t + i) // 9, (4 * t + i) % 9
                m0[
                    j // 2, q, (j % 2) * RANK : (j % 2 + 1) * RANK,
                    lane * LANES : (lane + 1) * LANES,
                ] = part[:, i * LANES : (i + 1) * LANES]
    grams = []
    for pair in range(2):
        gram = dot_t(m0[pair, 0], m0[pair, 0])
        for q in range(1, 4):
            gram += dot_t(m0[pair, q], m0[pair, q])
        grams.append(gram)
    for pair, combiner in enumerate(combiners(grams, mixers[0])):
        for q in range(4):
            m1[q, pair * RANK : (pair + 1) * RANK, :] = dot(combiner, m0[pair, q]).astype(BF16)

    own_terms.wait()
    core_copy.wait_recv()

    @pl.loop(0, 36)
    def _(i):
        ro[:, i] = (ro[:, i].astype(F32) + rc[:, i].astype(F32)).astype(BF16)

    y_copies = [
        send(ro.at[lax.rem(y + d, NY)], ry.at[d - 1], d, y_peers[d - 1]) for d in range(1, NY)
    ]

    gram = dot_t(m1[0], m1[0])
    for q in range(1, 4):
        gram += dot_t(m1[q], m1[q])
    (combiner,) = combiners([gram], mixers[0])
    ma[0] = dot(combiner, m1[x]).astype(BF16)

    def y_stage():
        for copy in y_copies:
            copy.wait_recv()

        @pl.loop(0, 36)
        def _(i):
            total = ro[y, i].astype(F32)
            for d in range(NY - 1):
                total += ry[d, i].astype(F32)
            w2[i] = total.astype(BF16)

        return [
            send(w2.at[pl.ds(lax.rem(x + d, NX) * 9, 9)], rx.at[d - 1], 3 + d, x_peers[d - 1])
            for d in range(1, NX)
        ]

    def x_stage():
        for copy in x_copies:
            copy.wait_recv()
        for pair in range(5):
            halves = []
            for t in (2 * pair, 2 * pair + 1):
                if t < TAPS:
                    total = w2[x * 9 + t].astype(F32)
                    for d in range(NX - 1):
                        total += rx[d, t].astype(F32)
                else:
                    total = jnp.zeros((64, LANES), F32)
                halves.append(total)
            turned = jnp.concatenate(halves, axis=0).T.astype(BF16)
            for k in range(NZ):
                wz[k, pair] = turned[k * 16 : (k + 1) * 16, :]
        return [
            send(wz.at[lax.rem(z + d, NZ)], rz.at[d - 1], 6 + d, z_peers[d - 1])
            for d in range(1, NZ)
        ]

    def flip(value, bit):
        return value + bit - 2 * bit * lax.rem(lax.div(value, bit), 2)

    levels = [
        (at(flip(z, 1), x, y, core), lax.rem(z, 2), 0),
        (at(flip(z, 2), x, y, core), lax.rem(lax.div(z, 2), 2), 0),
        (at(flip(z, 4), x, y, core), lax.div(z, 4), 0),
        (core_peer, core, 1),
        (at(z, x, flip(y, 1), core), lax.rem(y, 2), 1),
        (at(z, x, flip(y, 2), core), lax.div(y, 2), 1),
    ]
    for level, (peer, upper, which) in enumerate(levels):
        base = 14 + 5 * level
        slice_copy = send(ma.at[level], mb.at[level], base, peer)
        da[level] = carried_gram(combiner, gram)
        gram_copy = send(da.at[level], db.at[level], base + 1, peer)
        if level == 1:
            x_copies = y_stage()
        if level == 2:
            z_copies = x_stage()
        mix = mixers[which]
        mix = jnp.where(
            upper == 0, mix, jnp.concatenate([mix[:, RANK:], mix[:, :RANK]], axis=1)
        )
        slice_copy.wait_recv()
        cross = dot_t(ma[level], mb[level]).astype(BF16)
        po[level] = cross
        cross_copies = [
            send(po.at[level], pr.at[level, d - 1], base + 1 + d, x_peers[d - 1])
            for d in range(1, NX)
        ]
        gram_copy.wait_recv()
        for copy in cross_copies:
            copy.wait_recv()
        cross = cross.astype(F32)
        for d in range(NX - 1):
            cross += pr[level, d].astype(F32)
        gm[0:RANK, 0:RANK] = da[level]
        gm[0:RANK, RANK:] = cross
        gm[RANK:, 0:RANK] = cross.T
        gm[RANK:, RANK:] = db[level]
        gram = gm[...]
        (combiner,) = combiners([gram], mix)
        stacked = jnp.concatenate([ma[level], mb[level]], axis=0)
        ma[level + 1] = dot(combiner, stacked).astype(BF16)

    last = len(levels)
    own_rows = pl.ds(pl.multiple_of(col * 16, 16), 16)
    fr[0] = ma[last, own_rows, :]
    final_copies = [
        send(ma.at[last, own_rows], fr.at[d], 43 + d, x_peers[d - 1]) for d in range(1, NX)
    ]
    for copy in z_copies:
        copy.wait_recv()
    for pair in range(5):
        total = wz[z, pair].astype(F32)
        for d in range(NZ - 1):
            total += rz[d, pair].astype(F32)
        gk[2 * pair] = total[:, :64]
        if 2 * pair + 1 < TAPS:
            gk[2 * pair + 1] = total[:, 64:]
    for copy in final_copies:
        copy.wait_recv()
    k = lax.broadcasted_iota(jnp.int32, (QUART, 144), 0)
    j = lax.broadcasted_iota(jnp.int32, (QUART, 144), 1)
    chosen = jnp.where(k == j + lax.rem(row, 8) * 144, 1.0, 0.0).astype(BF16)
    held = fr[lax.rem(x - lax.div(z, 2) + NX, NX)]
    sketch[...] = dot(held, chosen).astype(BF16)
    for copy in started:
        copy.wait_send()


def tree_call(wt, bands, proj, mixers):
    vmem = pl.BlockSpec(memory_space=pltpu.VMEM)
    return pl.pallas_call(
        tree_kernel,
        in_specs=[pl.BlockSpec(memory_space=pl.ANY), vmem, vmem, vmem],
        out_specs=[vmem, vmem],
        out_shape=[
            jax.ShapeDtypeStruct((TAPS, 16, 64), F32),
            jax.ShapeDtypeStruct((16, 144), BF16),
        ],
        scratch_shapes=[
            pltpu.VMEM((NY, 36, 64, LANES), BF16),
            pltpu.VMEM((NY, 36, 64, LANES), BF16),
            pltpu.VMEM((NY - 1, 36, 64, LANES), BF16),
            pltpu.VMEM((36, 64, LANES), BF16),
            pltpu.VMEM((NX - 1, 9, 64, LANES), BF16),
            pltpu.VMEM((NZ, 5, 16, LANES), BF16),
            pltpu.VMEM((NZ - 1, 5, 16, LANES), BF16),
            pltpu.VMEM((2, 4, 2 * RANK, QUART), BF16),
            pltpu.VMEM((4, 2 * RANK, QUART), BF16),
            pltpu.VMEM((7, RANK, QUART), BF16),
            pltpu.VMEM((6, RANK, QUART), BF16),
            pltpu.VMEM((6, RANK, RANK), F32),
            pltpu.VMEM((6, RANK, RANK), F32),
            pltpu.VMEM((6, RANK, RANK), BF16),
            pltpu.VMEM((6, 3, RANK, RANK), BF16),
            pltpu.VMEM((4, 16, QUART), BF16),
            pltpu.VMEM((2 * RANK, 2 * RANK), F32),
            pltpu.SemaphoreType.DMA((1,)),
            pltpu.SemaphoreType.DMA((47,)),
            pltpu.SemaphoreType.DMA((47,)),
        ],
        compiler_params=pltpu.CompilerParams(
            collective_id=0, has_side_effects=True, vmem_limit_bytes=48 << 20
        ),
        name="merge_tree",
    )(wt, bands, proj, mixers)


def padded_2(x, sides, width):
    for axis, dim in sides:
        size, length = (lax.axis_size(axis), x.shape[dim])
        up = [(i, (i + 1) % size) for i in range(size - 1)]
        down = [(j, i) for i, j in up]
        last = lax.slice_in_dim(x, length - width, length, axis=dim)
        first = lax.slice_in_dim(x, 0, width, axis=dim)
        before = lax.ppermute(last, axis, up)
        after = lax.ppermute(first, axis, down)
        x = jnp.concatenate([before, x, after], axis=dim)
    return x


def shifted(padded):
    lead = padded.shape[:-3]
    rows, channels = padded.shape[-3], padded.shape[-1]
    return jnp.stack(
        [
            lax.slice_in_dim(padded, b, b + 32, axis=padded.ndim - 2).reshape(
                lead + (rows * 32, channels)
            )
            for b in range(3)
        ]
    )


def ring_gather(v):
    pieces = [v]
    for d in range(1, NX):
        moves = [(z * NX + (x + d) % NX, z * NX + x) for z in range(NZ) for x in range(NX)]
        pieces.append(lax.ppermute(v, "rows", moves))
    return jnp.stack(pieces)


def body(features, kernel, out_grad, projector, mixers):
    band_rows, band_cols, channels = features.shape
    pixels = band_rows * band_cols
    projectors = ring_gather(projector)
    padded = padded_2(features, (("rows", 0), ("cols", 1)), 1)
    grad_padded = padded_2(out_grad, (("rows", 0), ("cols", 1)), 1)
    bands = shifted(ring_gather(padded))
    output, grad_features, terms = local_call(
        shifted(padded),
        shifted(grad_padded),
        out_grad.reshape(pixels, channels).T,
        kernel.reshape(TAPS, channels, channels),
    )
    terms = terms.reshape(NY, NC, NX * TAPS, 64, LANES)
    grad_kernel, own_block = tree_call(terms, bands, projectors, mixers)
    shape = (band_rows, band_cols, channels)
    return (output.reshape(shape), grad_features.reshape(shape), grad_kernel, own_block)


def solution(mesh):
    in_specs = (P("rows", "cols", None), P(), P("rows", "cols", None), P("rows", "cols"), P())
    out_specs = (
        P("rows", "cols", None),
        P("rows", "cols", None),
        P(None, "rows", "cols"),
        P("cols", "rows"),
    )
    return jax.shard_map(body, mesh=mesh, in_specs=in_specs, out_specs=out_specs, check_vma=False)
```

time: 786 us -> 189 us (0.24); the launches traced: 777 us -> 188 us
  waiting for transfers between devices: 551 us -> 12.1 us
  Pallas kernels: 0 us -> 132 us
  matrix products: 86.2 us -> 0 us
  local copies, waits for them, and re-layouts: 40.5 us -> 8.4 us
  other arithmetic: 32.6 us -> 1.5 us
  between operations: 26.5 us -> 0.93 us
    reduce_scatter x1 -> x0, waiting for transfers between devices: 336 us -> none  [body(): lax.psum_scatter(flat_terms, ('rows', 'cols'), scatter_dimension=0, tiled...]
    ppermute x8 -> x6, waiting for transfers between devices: 190 us -> 9.65 us  [ring_gather(): pieces.append(lax.ppermute(v, 'rows', moves))]
    pallas_call x0 -> x2, Pallas kernels: none -> 132 us  [the longest x1 124 us: tree_call(): pl.pallas_call(tree_kernel, in_specs=[pl.BlockSpec(memory_space=pl.ANY),...]
    dot_general x124 -> x0, matrix products: 86.2 us -> none  [the longest x40 24.1 us: finish_merge(): jnp.dot(spread, square, precision=lax.Precision.HIGHEST)]
    ppermute x4, waiting for transfers between devices: 24.7 us -> 2.47 us  [padded_2(): after = lax.ppermute(first, axis, down)]
    select_n x8 -> x0, other arithmetic: 14.3 us -> none  [body(): jnp.where(is_lower, sketch, partner)]
    reshape x3 -> x1, local copies, waits for them, and re-layouts: 12.7 us -> 1.08 us  [body(): out_grad.reshape(pixels, channels)]
    another operation x1 -> x0, local copies, waits for them, and re-layouts: 11 us -> none  [body(): split_patches = patches.reshape(pixels, 9, row_count, channels // row_count)]
  transfers between devices with their start and end apart: 17 -> 14, of which waited for: 11 -> 3; matrix products, arithmetic and copies ran while one was open for 12% -> 2% of each run, Pallas kernels for 0% -> 4%
where the time goes in v1:
time: 189 us; the launch traced here: 188 us
  Pallas kernels  132 us (70%)
  starting transfers between devices  33.8 us (18%)
  waiting for transfers between devices  12.1 us (6%)
  local copies, waits for them, and re-layouts  8.4 us (4%)
    pallas_call x1, Pallas kernels, tree_call(): pl.pallas_call(tree_kernel, in_specs=[pl.BlockSpec(memory_space=pl.ANY),...  124 us
    ppermute x6, starting transfers between devices, ring_gather(): pieces.append(lax.ppermute(v, 'rows', moves))  13.6 us
    ppermute x4, starting transfers between devices, padded_2(): before = lax.ppermute(last, axis, up)  12.6 us
    ppermute x6, waiting for transfers between devices, ring_gather(): pieces.append(lax.ppermute(v, 'rows', moves))  9.65 us
    ppermute x4, starting transfers between devices, padded_2(): after = lax.ppermute(first, axis, down)  7.65 us
    pallas_call x1, Pallas kernels, local_call(): pl.pallas_call(local_kernel, grid=(TAPS,), in_specs=[whole(3, 320, CH), w...  7.15 us
    unnamed x16, local copies, waits for them, and re-layouts  4.81 us
  transfers between devices with their start and end apart: 14, of which 3 were waited for; matrix products, arithmetic and copies ran while one was open for 2% of the time, Pallas kernels for 4%

profile of v1, /device:TPU:8, one launch (start us, length us, event | category | flops | bytes accessed | tf_op | source)
XLA Modules:
  0.0 188.3 jit_solution(18200295655197433055)
XLA Ops:
  0.6 0.0 copy-start.3
  0.6 2.8 %collective-permute-start.11 = (bf16[128,256]{1,0:T(8,128)(2,1)}, bf16[128,256]{1,0:T(8,128)(2,1)S(1)}, u32[]{:S(2)}, u32[]{:S(2)}) collective-permute-start(bf16[128,256]{1,0:T(8,128)(2,1)} %param.8), channel_id=1, source_target_pairs={{8,0},{16,8},{24,16},{0,24},{40,32},{48,40},{56,48},{32,56},{72,64... | collective-permute-start | bytes 196616 | tf_op jit(solution)/shard_map/ppermute | solution.py:394
  3.5 0.8 collective-permute-start.12
  4.3 0.9 collective-permute-start.13
  5.2 0.8 fusion.5
  5.9 3.7 %collective-permute-start = (bf16[1,32,512]{2,1,0:T(8,128)(2,1)S(1)}, bf16[1,32,512]{2,1,0:T(8,128)(2,1)S(1)}, u32[]{:S(2)}, u32[]{:S(2)}) collective-permute-start(bf16[1,32,512]{2,1,0:T(8,128)(2,1)S(1)} %get-tuple-element.30), channel_id=1, source_target_pairs={{0,8},{8,16},{16,24},{24,32},{32,40},{40,48},{48,56},{56,64},{64,7... | collective-permute-start | bytes 98312 | tf_op jit(solution)/shard_map/ppermute | solution.py:371
  9.6 1.3 collective-permute-start.1
  10.9 0.8 fusion.4
  11.7 1.1 copy.10
  12.8 0.0 collective-permute-done
  12.8 4.5 %collective-permute-start.4 = (bf16[1,32,512]{2,1,0:T(8,128)(2,1)S(1)}, bf16[1,32,512]{2,1,0:T(8,128)(2,1)S(1)}, u32[]{:S(2)}, u32[]{:S(2)}) collective-permute-start(bf16[1,32,512]{2,1,0:T(8,128)(2,1)S(1)} %get-tuple-element.28), channel_id=1, source_target_pairs={{0,8},{8,16},{16,24},{24,32},{32,40},{40,48},{48,56},{56,64},{64,7... | collective-permute-start | bytes 98312 | tf_op jit(solution)/shard_map/ppermute | solution.py:371
  17.4 1.0 constant_dynamic-update-slice_fusion.1
  18.4 0.0 collective-permute-done.1
  18.4 1.3 collective-permute-start.5
  19.7 0.0 collective-permute-done.4
  19.7 1.9 %collective-permute-start.2 = (bf16[10,1,512]{2,1,0:T(2,128)(2,1)S(1)}, bf16[10,1,512]{2,1,0:T(2,128)(2,1)S(1)}, u32[]{:S(2)}, u32[]{:S(2)}) collective-permute-start(bf16[10,1,512]{2,1,0:T(2,128)(2,1)S(1)} %get-tuple-element.25), channel_id=1, source_target_pairs={{0,1},{1,2},{2,3},{3,4},{4,5},{5,6},{6,7},{8,9},{9,10},{10,11},{11... | collective-permute-start | bytes 30728 | tf_op jit(solution)/shard_map/ppermute | solution.py:371
  21.7 0.0 copy-done.3
  21.7 2.5 %collective-permute-done.5 = bf16[1,32,512]{2,1,0:T(8,128)(2,1)S(1)} collective-permute-done((bf16[1,32,512]{2,1,0:T(8,128)(2,1)S(1)}, bf16[1,32,512]{2,1,0:T(8,128)(2,1)S(1)}, u32[]{:S(2)}, u32[]{:S(2)}) %collective-permute-start.5) | collective-permute-done | bytes 32800 | tf_op jit(solution)/shard_map/ppermute | solution.py:372
  24.2 1.9 %collective-permute-start.3 = (bf16[10,1,512]{2,1,0:T(2,128)(2,1)S(1)}, bf16[10,1,512]{2,1,0:T(2,128)(2,1)S(1)}, u32[]{:S(2)}, u32[]{:S(2)}) collective-permute-start(bf16[10,1,512]{2,1,0:T(2,128)(2,1)S(1)} %get-tuple-element.26), channel_id=1, source_target_pairs={{1,0},{2,1},{3,2},{4,3},{5,4},{6,5},{7,6},{9,8},{10,9},{11,10},{12... | collective-permute-start | bytes 30728 | tf_op jit(solution)/shard_map/ppermute | solution.py:372
  26.2 0.0 collective-permute-done.2
  26.2 2.4 %collective-permute-start.6 = (bf16[10,1,512]{2,1,0:T(2,128)(2,1)S(1)}, bf16[10,1,512]{2,1,0:T(2,128)(2,1)S(1)}, u32[]{:S(2)}, u32[]{:S(2)}) collective-permute-start(bf16[10,1,512]{2,1,0:T(2,128)(2,1)S(1)} %get-tuple-element.21), channel_id=1, source_target_pairs={{0,1},{1,2},{2,3},{3,4},{4,5},{5,6},{6,7},{8,9},{9,10},{10,11},{11... | collective-permute-start | bytes 30728 | tf_op jit(solution)/shard_map/ppermute | solution.py:371
  28.6 0.0 collective-permute-done.3
  28.6 3.2 %collective-permute-start.7 = (bf16[10,1,512]{2,1,0:T(2,128)(2,1)S(1)}, bf16[10,1,512]{2,1,0:T(2,128)(2,1)S(1)}, u32[]{:S(2)}, u32[]{:S(2)}) collective-permute-start(bf16[10,1,512]{2,1,0:T(2,128)(2,1)S(1)} %get-tuple-element.22), channel_id=1, source_target_pairs={{1,0},{2,1},{3,2},{4,3},{5,4},{6,5},{7,6},{9,8},{10,9},{11,10},{12... | collective-permute-start | bytes 30728 | tf_op jit(solution)/shard_map/ppermute | solution.py:372
  31.8 0.2 pad_maximum_fusion.8
  32.0 0.0 copy-start.2
  32.0 0.1 pad_maximum_fusion.2.xs
  32.1 0.2 fusion
  32.3 0.0 collective-permute-done.6
  32.3 7.1 %collective-permute-start.8 = (bf16[10,34,512]{2,1,0:T(8,128)(2,1)S(1)}, bf16[10,34,512]{2,1,0:T(8,128)(2,1)S(1)}, u32[]{:S(2)}, u32[]{:S(2)}) collective-permute-start(bf16[10,34,512]{2,1,0:T(8,128)(2,1)S(1)} %get-tuple-element.18), channel_id=1, source_target_pairs={{8,0},{16,8},{24,16},{0,24},{40,32},{48,40},{56,48},{32,56},{72,64... | collective-permute-start | bytes 1044488 | tf_op jit(solution)/shard_map/ppermute | solution.py:394
  39.4 0.0 collective-permute-done.7
  39.4 0.0 collective-permute-start.9
  39.4 0.2 pad_maximum_fusion.6
  39.6 0.1 pad_maximum_fusion.3.gs
  39.7 0.0 collective-permute-done.11
  39.7 2.0 %collective-permute-start.10 = (bf16[10,34,512]{2,1,0:T(8,128)(2,1)S(1)}, bf16[10,34,512]{2,1,0:T(8,128)(2,1)S(1)}, u32[]{:S(2)}, u32[]{:S(2)}) collective-permute-start(bf16[10,34,512]{2,1,0:T(8,128)(2,1)S(1)} %get-tuple-element.18), channel_id=1, source_target_pairs={{24,0},{0,8},{8,16},{16,24},{56,32},{32,40},{40,48},{48,56},{88,64... | collective-permute-start | bytes 1044488 | tf_op jit(solution)/shard_map/ppermute | solution.py:394
  41.7 0.0 copy-done.2
  41.7 0.0 copy-start.4
  41.7 7.1 %conv_terms.1 = (bf16[256,512]{1,0:T(8,128)(2,1)}, bf16[256,512]{1,0:T(8,128)(2,1)}, bf16[4,2,4,9,64,128]{5,4,3,2,1,0:T(8,128)(2,1)S(1)}) custom-call(bf16[3,320,512]{2,1,0:T(8,128)(2,1)S(1)} %pad_maximum_fusion.2.xs, bf16[3,320,512]{2,1,0:T(8,128)(2,1)S(1)} %pad_maximum_fusion.3.gs, bf16[512,256]{1,0:T(8,128)(2,1)S(1)} %bitcast.25, ...), custom_call_target="tpu_custom_call" | custom-call | flops 3623878656 | bytes 11534336 | tf_op jit(solution)/shard_map/conv_terms/pallas_call | solution.py:69
  48.8 0.0 copy-start
  48.8 2.1 %copy-done = bf16[4,2,4,9,64,128]{5,4,3,2,1,0:T(8,128)(2,1)} copy-done((bf16[4,2,4,9,64,128]{5,4,3,2,1,0:T(8,128)(2,1)}, bf16[4,2,4,9,64,128]{5,4,3,2,1,0:T(8,128)(2,1)S(1)}, u32[]{:S(2)}) %copy-start) | copy-done | bytes 4718616
  51.0 0.0 collective-permute-done.12
  51.0 0.0 collective-permute-done.13
  51.0 0.0 copy-done.4
  51.0 5.9 %collective-permute-done.8 = bf16[10,34,512]{2,1,0:T(8,128)(2,1)S(1)} collective-permute-done((bf16[10,34,512]{2,1,0:T(8,128)(2,1)S(1)}, bf16[10,34,512]{2,1,0:T(8,128)(2,1)S(1)}, u32[]{:S(2)}, u32[]{:S(2)}) %collective-permute-start.8) | collective-permute-done | bytes 348192 | tf_op jit(solution)/shard_map/ppermute | solution.py:394
  57.0 0.0 collective-permute-done.9
  57.0 3.7 %collective-permute-done.10 = bf16[10,34,512]{2,1,0:T(8,128)(2,1)S(1)} collective-permute-done((bf16[10,34,512]{2,1,0:T(8,128)(2,1)S(1)}, bf16[10,34,512]{2,1,0:T(8,128)(2,1)S(1)}, u32[]{:S(2)}, u32[]{:S(2)}) %collective-permute-start.10) | collective-permute-done | bytes 348192 | tf_op jit(solution)/shard_map/ppermute | solution.py:394
  60.7 0.2 pad_maximum_fusion.1
  60.9 0.9 fusion.1
  61.8 0.0 copy-start.1
  61.8 0.5 pad_maximum_fusion.bands
  62.3 0.4 copy-done.1
  62.7 124.4 %merge_tree.1 = (f32[9,16,64]{2,1,0:T(8,128)S(1)}, bf16[16,144]{1,0:T(8,128)(2,1)S(1)}) custom-call(bf16[4,2,36,64,128]{4,3,2,1,0:T(8,128)(2,1)} %bitcast.24, bf16[3,4,320,512]{3,2,1,0:T(8,128)(2,1)S(1)} %pad_maximum_fusion.bands, bf16[4,128,256]{2,1,0:T(8,128)(2,1)S(1)} %pad_maximum_fusion.9.proj, bf16[2,128,256]{2,1,0:T(8,128)(2,1)S(1)} %copy-done.1), custom_call_target="tpu_custom_call" | custom-call | tf_op jit(solution)/shard_map/merge_tree/pallas_call | solution.py:327
  187.1 0.6 copy.17
  187.7 0.6 copy.18
  (8 shorter events, 0.1 us)
Async XLA Ops:
  0.6 21.1 %copy-start.3 = (bf16[8,32,512]{2,1,0:T(8,128)(2,1)S(1)}, bf16[8,32,512]{2,1,0:T(8,128)(2,1)}, u32[]{:S(2)}) copy-start(bf16[8,32,512]{2,1,0:T(8,128)(2,1)} %param.7) | copy-start | bytes 786436
  0.6 39.0 %collective-permute-start.11 = (bf16[128,256]{1,0:T(8,128)(2,1)}, bf16[128,256]{1,0:T(8,128)(2,1)S(1)}, u32[]{:S(2)}, u32[]{:S(2)}) collective-permute-start(bf16[128,256]{1,0:T(8,128)(2,1)} %param.8), channel_id=1, source_target_pairs={{8,0},{16,8},{24,16},{0,24},{40,32},{48,40},{56,48},{32,56},{72,64... | collective-permute-start | bytes 196616 | tf_op jit(solution)/shard_map/ppermute | solution.py:394
  3.5 47.5 %collective-permute-start.12 = (bf16[128,256]{1,0:T(8,128)(2,1)}, bf16[128,256]{1,0:T(8,128)(2,1)S(1)}, u32[]{:S(2)}, u32[]{:S(2)}) collective-permute-start(bf16[128,256]{1,0:T(8,128)(2,1)} %param.8), channel_id=1, source_target_pairs={{16,0},{24,8},{0,16},{8,24},{48,32},{56,40},{32,48},{40,56},{80,64... | collective-permute-start | bytes 196616 | tf_op jit(solution)/shard_map/ppermute | solution.py:394
  4.3 46.7 %collective-permute-start.13 = (bf16[128,256]{1,0:T(8,128)(2,1)}, bf16[128,256]{1,0:T(8,128)(2,1)S(1)}, u32[]{:S(2)}, u32[]{:S(2)}) collective-permute-start(bf16[128,256]{1,0:T(8,128)(2,1)} %param.8), channel_id=1, source_target_pairs={{24,0},{0,8},{8,16},{16,24},{56,32},{32,40},{40,48},{48,56},{88,64... | collective-permute-start | bytes 196616 | tf_op jit(solution)/shard_map/ppermute | solution.py:394
  5.9 6.9 %collective-permute-start = (bf16[1,32,512]{2,1,0:T(8,128)(2,1)S(1)}, bf16[1,32,512]{2,1,0:T(8,128)(2,1)S(1)}, u32[]{:S(2)}, u32[]{:S(2)}) collective-permute-start(bf16[1,32,512]{2,1,0:T(8,128)(2,1)S(1)} %get-tuple-element.30), channel_id=1, source_target_pairs={{0,8},{8,16},{16,24},{24,32},{32,40},{40,48},{48,56},{56,64},{64,7... | collective-permute-start | bytes 98312 | tf_op jit(solution)/shard_map/ppermute | solution.py:371
  9.6 8.7 %collective-permute-start.1 = (bf16[1,32,512]{2,1,0:T(8,128)(2,1)S(1)}, bf16[1,32,512]{2,1,0:T(8,128)(2,1)S(1)}, u32[]{:S(2)}, u32[]{:S(2)}) collective-permute-start(bf16[1,32,512]{2,1,0:T(8,128)(2,1)S(1)} %get-tuple-element.29), channel_id=1, source_target_pairs={{8,0},{16,8},{24,16},{32,24},{40,32},{48,40},{56,48},{64,56},{72,6... | collective-permute-start | bytes 98312 | tf_op jit(solution)/shard_map/ppermute | solution.py:372
  12.8 6.9 %collective-permute-start.4 = (bf16[1,32,512]{2,1,0:T(8,128)(2,1)S(1)}, bf16[1,32,512]{2,1,0:T(8,128)(2,1)S(1)}, u32[]{:S(2)}, u32[]{:S(2)}) collective-permute-start(bf16[1,32,512]{2,1,0:T(8,128)(2,1)S(1)} %get-tuple-element.28), channel_id=1, source_target_pairs={{0,8},{8,16},{16,24},{24,32},{32,40},{40,48},{48,56},{56,64},{64,7... | collective-permute-start | bytes 98312 | tf_op jit(solution)/shard_map/ppermute | solution.py:371
  18.4 5.8 %collective-permute-start.5 = (bf16[1,32,512]{2,1,0:T(8,128)(2,1)S(1)}, bf16[1,32,512]{2,1,0:T(8,128)(2,1)S(1)}, u32[]{:S(2)}, u32[]{:S(2)}) collective-permute-start(bf16[1,32,512]{2,1,0:T(8,128)(2,1)S(1)} %get-tuple-element.27), channel_id=1, source_target_pairs={{8,0},{16,8},{24,16},{32,24},{40,32},{48,40},{56,48},{64,56},{72,6... | collective-permute-start | bytes 98312 | tf_op jit(solution)/shard_map/ppermute | solution.py:372
  19.7 6.4 %collective-permute-start.2 = (bf16[10,1,512]{2,1,0:T(2,128)(2,1)S(1)}, bf16[10,1,512]{2,1,0:T(2,128)(2,1)S(1)}, u32[]{:S(2)}, u32[]{:S(2)}) collective-permute-start(bf16[10,1,512]{2,1,0:T(2,128)(2,1)S(1)} %get-tuple-element.25), channel_id=1, source_target_pairs={{0,1},{1,2},{2,3},{3,4},{4,5},{5,6},{6,7},{8,9},{9,10},{10,11},{11... | collective-permute-start | bytes 30728 | tf_op jit(solution)/shard_map/ppermute | solution.py:371
  24.2 4.4 %collective-permute-start.3 = (bf16[10,1,512]{2,1,0:T(2,128)(2,1)S(1)}, bf16[10,1,512]{2,1,0:T(2,128)(2,1)S(1)}, u32[]{:S(2)}, u32[]{:S(2)}) collective-permute-start(bf16[10,1,512]{2,1,0:T(2,128)(2,1)S(1)} %get-tuple-element.26), channel_id=1, source_target_pairs={{1,0},{2,1},{3,2},{4,3},{5,4},{6,5},{7,6},{9,8},{10,9},{11,10},{12... | collective-permute-start | bytes 30728 | tf_op jit(solution)/shard_map/ppermute | solution.py:372
  26.2 6.1 %collective-permute-start.6 = (bf16[10,1,512]{2,1,0:T(2,128)(2,1)S(1)}, bf16[10,1,512]{2,1,0:T(2,128)(2,1)S(1)}, u32[]{:S(2)}, u32[]{:S(2)}) collective-permute-start(bf16[10,1,512]{2,1,0:T(2,128)(2,1)S(1)} %get-tuple-element.21), channel_id=1, source_target_pairs={{0,1},{1,2},{2,3},{3,4},{4,5},{5,6},{6,7},{8,9},{9,10},{10,11},{11... | collective-permute-start | bytes 30728 | tf_op jit(solution)/shard_map/ppermute | solution.py:371
  28.6 10.8 %collective-permute-start.7 = (bf16[10,1,512]{2,1,0:T(2,128)(2,1)S(1)}, bf16[10,1,512]{2,1,0:T(2,128)(2,1)S(1)}, u32[]{:S(2)}, u32[]{:S(2)}) collective-permute-start(bf16[10,1,512]{2,1,0:T(2,128)(2,1)S(1)} %get-tuple-element.22), channel_id=1, source_target_pairs={{1,0},{2,1},{3,2},{4,3},{5,4},{6,5},{7,6},{9,8},{10,9},{11,10},{12... | collective-permute-start | bytes 30728 | tf_op jit(solution)/shard_map/ppermute | solution.py:372
  32.0 9.7 %copy-start.2 = (bf16[4608,512]{1,0:T(8,128)(2,1)S(1)}, bf16[4608,512]{1,0:T(8,128)(2,1)}, u32[]{:S(2)}) copy-start(bf16[4608,512]{1,0:T(8,128)(2,1)} %param.6) | copy-start | bytes 14155780
  32.3 24.7 %collective-permute-start.8 = (bf16[10,34,512]{2,1,0:T(8,128)(2,1)S(1)}, bf16[10,34,512]{2,1,0:T(8,128)(2,1)S(1)}, u32[]{:S(2)}, u32[]{:S(2)}) collective-permute-start(bf16[10,34,512]{2,1,0:T(8,128)(2,1)S(1)} %get-tuple-element.18), channel_id=1, source_target_pairs={{8,0},{16,8},{24,16},{0,24},{40,32},{48,40},{56,48},{32,56},{72,64... | collective-permute-start | bytes 1044488 | tf_op jit(solution)/shard_map/ppermute | solution.py:394
  39.4 17.6 %collective-permute-start.9 = (bf16[10,34,512]{2,1,0:T(8,128)(2,1)S(1)}, bf16[10,34,512]{2,1,0:T(8,128)(2,1)S(1)}, u32[]{:S(2)}, u32[]{:S(2)}) collective-permute-start(bf16[10,34,512]{2,1,0:T(8,128)(2,1)S(1)} %get-tuple-element.18), channel_id=1, source_target_pairs={{16,0},{24,8},{0,16},{8,24},{48,32},{56,40},{32,48},{40,56},{80,64... | collective-permute-start | bytes 1044488 | tf_op jit(solution)/shard_map/ppermute | solution.py:394
  39.7 21.0 %collective-permute-start.10 = (bf16[10,34,512]{2,1,0:T(8,128)(2,1)S(1)}, bf16[10,34,512]{2,1,0:T(8,128)(2,1)S(1)}, u32[]{:S(2)}, u32[]{:S(2)}) collective-permute-start(bf16[10,34,512]{2,1,0:T(8,128)(2,1)S(1)} %get-tuple-element.18), channel_id=1, source_target_pairs={{24,0},{0,8},{8,16},{16,24},{56,32},{32,40},{40,48},{48,56},{88,64... | collective-permute-start | bytes 1044488 | tf_op jit(solution)/shard_map/ppermute | solution.py:394
  41.7 9.3 %copy-start.4 = (bf16[128,256]{1,0:T(8,128)(2,1)S(1)}, bf16[128,256]{1,0:T(8,128)(2,1)}, u32[]{:S(2)}) copy-start(bf16[128,256]{1,0:T(8,128)(2,1)} %param.8) | copy-start | bytes 196612
  48.8 2.2 %copy-start = (bf16[4,2,4,9,64,128]{5,4,3,2,1,0:T(8,128)(2,1)}, bf16[4,2,4,9,64,128]{5,4,3,2,1,0:T(8,128)(2,1)S(1)}, u32[]{:S(2)}) copy-start(bf16[4,2,4,9,64,128]{5,4,3,2,1,0:T(8,128)(2,1)S(1)} %get-tuple-element.11) | copy-start | bytes 14155780
  61.8 0.9 copy-start.1

commit v2 on v1

--- a/solution.py
+++ b/solution.py
@@ -30,74 +30,6 @@
     return high, (v - high.astype(F32)).astype(BF16)
 
 
-def local_kernel(xs, gs, ogt, kern, out, gfeat, wt, acc_o, acc_g, xsp):
-    t = pl.program_id(0)
-
-    @pl.when(t == 0)
-    def _():
-        acc_o[...] = jnp.zeros_like(acc_o)
-        acc_g[...] = jnp.zeros_like(acc_g)
-        ci = lax.broadcasted_iota(jnp.int32, (CH, CH), 0)
-        to = lax.broadcasted_iota(jnp.int32, (CH, CH), 1)
-        source = lax.rem(lax.div(to, 16), NZ) * 64 + lax.div(to, 128) * 16 + lax.rem(to, 16)
-        perm = jnp.where(ci == source, 1.0, 0.0).astype(BF16)
-        for b in range(3):
-            xsp[b] = dot(xs[b], perm).astype(BF16)
-
-    a = lax.div(t, 3)
-    b = lax.rem(t, 3)
-    start = pl.multiple_of(a * 32, 32)
-    back = pl.multiple_of((2 - a) * 32, 32)
-    weights = kern[0]
-    acc_o[...] += dot(xs[b, pl.ds(start, 256), :], weights)
-    acc_g[...] += dot_t(gs[2 - b, pl.ds(back, 256), :], weights)
-    terms = dot(ogt[...], xsp[b, pl.ds(start, 256), :]).astype(BF16)
-    for y in range(NY):
-        for core in range(NC):
-            for x in range(NX):
-                at = (y * NC + core) * 64
-                wt[y, core, x, 0] = terms[at : at + 64, x * LANES : (x + 1) * LANES]
-
-    @pl.when(t == TAPS - 1)
-    def _():
-        out[...] = acc_o[...].astype(BF16)
-        gfeat[...] = acc_g[...].astype(BF16)
-
-
-def local_call(xs, gs, ogt, kernel):
-    whole = lambda *shape: pl.BlockSpec(shape, lambda t: (0,) * len(shape))
-    return pl.pallas_call(
-        local_kernel,
-        grid=(TAPS,),
-        in_specs=[
-            whole(3, 320, CH),
-            whole(3, 320, CH),
-            whole(CH, 256),
-            pl.BlockSpec((1, CH, CH), lambda t: (t, 0, 0)),
-        ],
-        out_specs=[
-            whole(256, CH),
-            whole(256, CH),
-            pl.BlockSpec((NY, NC, NX, 1, 64, LANES), lambda t: (0, 0, 0, t, 0, 0)),
-        ],
-        out_shape=[
-            jax.ShapeDtypeStruct((256, CH), BF16),
-            jax.ShapeDtypeStruct((256, CH), BF16),
-            jax.ShapeDtypeStruct((NY, NC, NX, TAPS, 64, LANES), BF16),
-        ],
-        scratch_shapes=[
-            pltpu.VMEM((256, CH), F32),
-            pltpu.VMEM((256, CH), F32),
-            pltpu.VMEM((3, 320, CH), BF16),
-        ],
-        compiler_params=pltpu.CompilerParams(vmem_limit_bytes=32 << 20),
-        cost_estimate=pl.CostEstimate(
-            flops=3 * 2 * 256 * 4608 * 512, bytes_accessed=11 << 20, transcendentals=0
-        ),
-        name="conv_terms",
-    )(xs, gs, ogt, kernel)
-
-
 def start_spread(gram):
     size = gram.shape[0]
     i = lax.broadcasted_iota(jnp.int32, (size, size), 0)
@@ -133,11 +65,25 @@
     return dot_t(high, combiner) + dot_t(low, combiner)
 
 
-def tree_kernel(
-    wt, bands, proj, mixers, gk, sketch,
+def shift_columns(held, edges, slot_at):
+    row_in = lax.broadcasted_iota(jnp.int32, (32, CH), 0)
+    left, right = edges
+    for h in range(10):
+        rows = slice(h * 32, h * 32 + 32)
+        mid = held[slot_at + (1, rows)].astype(F32)
+        before = jnp.where(row_in == 0, left[h : h + 1], pltpu.roll(mid, 1, 0))
+        after = jnp.where(row_in == 31, right[h : h + 1], pltpu.roll(mid, 31, 0))
+        held[slot_at + (0, rows)] = before.astype(BF16)
+        held[slot_at + (2, rows)] = after.astype(BF16)
+
+
+def step_kernel(
+    feat, grad, strips, kern, proj, mixers, out, gfeat, gk, sketch,
+    bx, be, pj, gs, edge, line, xsp, ogt, kv, wt, acc,
     ro, rc, ry, w2, rx, wz, rz, m0, m1, ma, mb, da, db, po, pr, fr, gm, lsem, ssem, rsem,
 ):
     row, col = lax.axis_index("rows"), lax.axis_index("cols")
+    n_rows, n_cols = NX * NZ, NY * NC
     z, x = lax.div(row, NX), lax.rem(row, NX)
     y, core = lax.div(col, NC), lax.rem(col, NC)
 
@@ -148,11 +94,26 @@
     y_peers = [at(z, x, lax.rem(y + d, NY), core) for d in range(1, NY)]
     z_peers = [at(lax.rem(z + d, NZ), x, y, core) for d in range(1, NZ)]
     core_peer = at(z, x, y, 1 - core)
+    above, below = lax.rem(row + n_rows - 1, n_rows), lax.rem(row + 1, n_rows)
+    before, after = lax.rem(col + n_cols - 1, n_cols), lax.rem(col + 1, n_cols)
+    around = [(r, c) for c in (before, after) for r in (above, row, below)]
+    around += [(above, col), (below, col)]
+
+    def fetch(src, dst, i):
+        copy = pltpu.make_async_copy(src, dst, lsem.at[i])
+        copy.start()
+        return copy
+
+    own_band = fetch(feat, bx.at[0, 1, 32:288], 0)
+    own_grad = fetch(grad, gs.at[1, 32:288], 1)
+    own_proj = fetch(proj, pj.at[0], 2)
+    weights = fetch(kern, kv, 3)
 
     barrier = pltpu.get_barrier_semaphore()
-    peers = x_peers + y_peers + z_peers + [core_peer]
+    peers = x_peers + y_peers + z_peers + [core_peer] + around
     for peer in peers:
         pl.semaphore_signal(barrier, inc=1, device_id=peer, device_id_type=MESH)
+    pl.semaphore_wait(barrier, len(peers))
 
     started = []
 
@@ -169,17 +130,87 @@
         started.append(copy)
         return copy
 
-    own_terms = pltpu.make_async_copy(wt.at[:, core], ro, lsem.at[0])
-    own_terms.start()
-    pl.semaphore_wait(barrier, len(peers))
+    halo = []
+    for k, r in enumerate((below, row, above)):
+        halo.append(send(strips.at[0], edge.at[1, k], 47 + k, (r, before)))
+        halo.append(send(strips.at[1], edge.at[0, k], 50 + k, (r, after)))
+    halo.append(send(feat.at[224:256], bx.at[0, 1, 0:32], 53, (below, col)))
+    halo.append(send(feat.at[0:32], bx.at[0, 1, 288:320], 54, (above, col)))
+    halo.append(send(grad.at[224:256], gs.at[1, 0:32], 55, (below, col)))
+    halo.append(send(grad.at[0:32], gs.at[1, 288:320], 56, (above, col)))
+    main = [
+        (
+            send(feat, bx.at[d, 1, 32:288], 56 + d, x_peers[d - 1]),
+            send(proj, pj.at[d], 59 + d, x_peers[d - 1]),
+        )
+        for d in range(1, NX)
+    ]
+    for copy in (own_band, own_grad, own_proj):
+        copy.wait()
+    ogt[...] = gs[1, 32:288].astype(F32).T.astype(BF16)
+    for copy in halo:
+        copy.wait_recv()
+
+    def kept(value, outside):
+        return jnp.where(outside, jnp.zeros_like(value), value)
+
+    top, bottom = row == 0, row == n_rows - 1
+    for held in (bx.at[0, 1], gs.at[1]):
+        held[0:32] = kept(held[0:32], top)
+        held[288:320] = kept(held[288:320], bottom)
+    line[...] = jnp.zeros_like(line)
+    for side, outside in enumerate((col == 0, col == n_cols - 1)):
+        up, mid, down = [kept(edge[side, k].astype(F32), outside) for k in range(3)]
+        for which in range(2):
+            rows = 8 * which
+            line[which, side, 0:1] = kept(up[rows + 7 : rows + 8], top)
+            line[which, side, 1:9] = mid[rows : rows + 8]
+            line[which, side, 9:10] = kept(down[rows : rows + 1], bottom)
+    be[0] = line[0].astype(BF16)
+    ends = [
+        (
+            send(bx.at[0, 1, 0:32], bx.at[d, 1, 0:32], 62 + d, x_peers[d - 1]),
+            send(bx.at[0, 1, 288:320], bx.at[d, 1, 288:320], 65 + d, x_peers[d - 1]),
+            send(be.at[0], be.at[d], 68 + d, x_peers[d - 1]),
+        )
+        for d in range(1, NX)
+    ]
+    shift_columns(bx, (line[0, 0], line[0, 1]), (0,))
+
+    ci = lax.broadcasted_iota(jnp.int32, (CH, CH), 0)
+    to = lax.broadcasted_iota(jnp.int32, (CH, CH), 1)
+    source = lax.rem(lax.div(to, 16), NZ) * 64 + lax.div(to, LANES) * 16 + lax.rem(to, 16)
+    perm = jnp.where(ci == source, 1.0, 0.0).astype(BF16)
+    for b in range(3):
+        xsp[b] = dot(bx[0, b], perm).astype(BF16)
+
+    @pl.loop(0, TAPS)
+    def _(t):
+        start = pl.multiple_of(lax.div(t, 3) * 32, 32)
+        terms = dot(ogt[...], xsp[lax.rem(t, 3), pl.ds(start, 256), :]).astype(BF16)
+        for yy in range(NY):
+            for cc in range(NC):
+                first = (yy * NC + cc) * 64
+                for xx in range(NX):
+                    wt[yy, cc, xx * TAPS + t] = terms[
+                        first : first + 64, xx * LANES : (xx + 1) * LANES
+                    ]
+
     core_copy = send(wt.at[:, 1 - core], rc, 0, core_peer)
+    shift_columns(gs, (line[1, 0], line[1, 1]), ())
+
+    for d in range(1, NX):
+        for copy in main[d - 1] + ends[d - 1]:
+            copy.wait_recv()
+        edges = be[d].astype(F32)
+        shift_columns(bx, (edges[0], edges[1]), (d,))
 
     for j in range(NX):
-        slot = lax.rem(j - x + NX, NX)
-        p = proj[slot]
+        slot = lax.rem(x - j + NX, NX)
+        p = pj[slot]
         for t in range(TAPS):
             a, b = t // 3, t % 3
-            part = dot(p, bands[b, slot, a * 32 : a * 32 + 256, :]).astype(BF16)
+            part = dot(p, bx[slot, b, a * 32 : a * 32 + 256, :]).astype(BF16)
             for i in range(4):
                 q, lane = (4 * t + i) // 9, (4 * t + i) % 9
                 m0[
@@ -196,22 +227,44 @@
         for q in range(4):
             m1[q, pair * RANK : (pair + 1) * RANK, :] = dot(combiner, m0[pair, q]).astype(BF16)
 
-    own_terms.wait()
-    core_copy.wait_recv()
-
-    @pl.loop(0, 36)
-    def _(i):
-        ro[:, i] = (ro[:, i].astype(F32) + rc[:, i].astype(F32)).astype(BF16)
-
-    y_copies = [
-        send(ro.at[lax.rem(y + d, NY)], ry.at[d - 1], d, y_peers[d - 1]) for d in range(1, NY)
-    ]
-
     gram = dot_t(m1[0], m1[0])
     for q in range(1, 4):
         gram += dot_t(m1[q], m1[q])
     (combiner,) = combiners([gram], mixers[0])
     ma[0] = dot(combiner, m1[x]).astype(BF16)
+
+    def core_stage():
+        core_copy.wait_recv()
+
+        @pl.loop(0, 36)
+        def _(i):
+            ro[:, i] = (wt[:, core, i].astype(F32) + rc[:, i].astype(F32)).astype(BF16)
+
+        return [
+            send(ro.at[lax.rem(y + d, NY)], ry.at[d - 1], d, y_peers[d - 1])
+            for d in range(1, NY)
+        ]
+
+    def forward():
+        weights.wait()
+        acc[...] = jnp.zeros_like(acc)
+
+        @pl.loop(0, TAPS)
+        def _(t):
+            start = pl.multiple_of(lax.div(t, 3) * 32, 32)
+            acc[...] += dot(bx[0, lax.rem(t, 3), pl.ds(start, 256), :], kv[t])
+
+        out[...] = acc[...].astype(BF16)
+
+    def backward():
+        acc[...] = jnp.zeros_like(acc)
+
+        @pl.loop(0, TAPS)
+        def _(t):
+            start = pl.multiple_of((2 - lax.div(t, 3)) * 32, 32)
+            acc[...] += dot_t(gs[2 - lax.rem(t, 3), pl.ds(start, 256), :], kv[t])
+
+        gfeat[...] = acc[...].astype(BF16)
 
     def y_stage():
         for copy in y_copies:
@@ -266,9 +319,14 @@
         slice_copy = send(ma.at[level], mb.at[level], base, peer)
         da[level] = carried_gram(combiner, gram)
         gram_copy = send(da.at[level], db.at[level], base + 1, peer)
+        if level == 0:
+            y_copies = core_stage()
+            forward()
         if level == 1:
+            backward()
+        if level == 2:
             x_copies = y_stage()
-        if level == 2:
+        if level == 4:
             z_copies = x_stage()
         mix = mixers[which]
         mix = jnp.where(
@@ -322,17 +380,30 @@
         copy.wait_send()
 
 
-def tree_call(wt, bands, proj, mixers):
+def step_call(feat, grad, strips, kern, proj, mixers):
     vmem = pl.BlockSpec(memory_space=pltpu.VMEM)
     return pl.pallas_call(
-        tree_kernel,
-        in_specs=[pl.BlockSpec(memory_space=pl.ANY), vmem, vmem, vmem],
-        out_specs=[vmem, vmem],
+        step_kernel,
+        in_specs=[pl.BlockSpec(memory_space=pl.ANY)] * 5 + [vmem],
+        out_specs=[vmem] * 4,
         out_shape=[
+            jax.ShapeDtypeStruct((256, CH), BF16),
+            jax.ShapeDtypeStruct((256, CH), BF16),
             jax.ShapeDtypeStruct((TAPS, 16, 64), F32),
             jax.ShapeDtypeStruct((16, 144), BF16),
         ],
         scratch_shapes=[
+            pltpu.VMEM((NX, 3, 320, CH), BF16),
+            pltpu.VMEM((NX, 2, 16, CH), BF16),
+            pltpu.VMEM((NX, RANK, 256), BF16),
+            pltpu.VMEM((3, 320, CH), BF16),
+            pltpu.VMEM((2, 3, 16, CH), BF16),
+            pltpu.VMEM((2, 2, 16, CH), F32),
+            pltpu.VMEM((3, 320, CH), BF16),
+            pltpu.VMEM((CH, 256), BF16),
+            pltpu.VMEM((TAPS, CH, CH), BF16),
+            pltpu.VMEM((NY, NC, 36, 64, LANES), BF16),
+            pltpu.VMEM((256, CH), F32),
             pltpu.VMEM((NY, 36, 64, LANES), BF16),
             pltpu.VMEM((NY, 36, 64, LANES), BF16),
             pltpu.VMEM((NY - 1, 36, 64, LANES), BF16),
@@ -350,67 +421,34 @@
             pltpu.VMEM((6, 3, RANK, RANK), BF16),
             pltpu.VMEM((4, 16, QUART), BF16),
             pltpu.VMEM((2 * RANK, 2 * RANK), F32),
-            pltpu.SemaphoreType.DMA((1,)),
-            pltpu.SemaphoreType.DMA((47,)),
-            pltpu.SemaphoreType.DMA((47,)),
+            pltpu.SemaphoreType.DMA((4,)),
+            pltpu.SemaphoreType.DMA((72,)),
+            pltpu.SemaphoreType.DMA((72,)),
         ],
         compiler_params=pltpu.CompilerParams(
-            collective_id=0, has_side_effects=True, vmem_limit_bytes=48 << 20
+            collective_id=0, has_side_effects=True, vmem_limit_bytes=56 << 20
         ),
-        name="merge_tree",
-    )(wt, bands, proj, mixers)
-
-
-def padded_2(x, sides, width):
-    for axis, dim in sides:
-        size, length = (lax.axis_size(axis), x.shape[dim])
-        up = [(i, (i + 1) % size) for i in range(size - 1)]
-        down = [(j, i) for i, j in up]
-        last = lax.slice_in_dim(x, length - width, length, axis=dim)
-        first = lax.slice_in_dim(x, 0, width, axis=dim)
-        before = lax.ppermute(last, axis, up)
-        after = lax.ppermute(first, axis, down)
-        x = jnp.concatenate([before, x, after], axis=dim)
-    return x
-
-
-def shifted(padded):
-    lead = padded.shape[:-3]
-    rows, channels = padded.shape[-3], padded.shape[-1]
-    return jnp.stack(
+        name="conv_step",
+    )(feat, grad, strips, kern, proj, mixers)
+
+
+def body(features, kernel, out_grad, projector, mixers):
+    shape = features.shape
+    channels = shape[2]
+    strips = jnp.stack(
         [
-            lax.slice_in_dim(padded, b, b + 32, axis=padded.ndim - 2).reshape(
-                lead + (rows * 32, channels)
-            )
-            for b in range(3)
+            jnp.concatenate([features[:, w], out_grad[:, w]], axis=0)
+            for w in (0, shape[1] - 1)
         ]
     )
-
-
-def ring_gather(v):
-    pieces = [v]
-    for d in range(1, NX):
-        moves = [(z * NX + (x + d) % NX, z * NX + x) for z in range(NZ) for x in range(NX)]
-        pieces.append(lax.ppermute(v, "rows", moves))
-    return jnp.stack(pieces)
-
-
-def body(features, kernel, out_grad, projector, mixers):
-    band_rows, band_cols, channels = features.shape
-    pixels = band_rows * band_cols
-    projectors = ring_gather(projector)
-    padded = padded_2(features, (("rows", 0), ("cols", 1)), 1)
-    grad_padded = padded_2(out_grad, (("rows", 0), ("cols", 1)), 1)
-    bands = shifted(ring_gather(padded))
-    output, grad_features, terms = local_call(
-        shifted(padded),
-        shifted(grad_padded),
-        out_grad.reshape(pixels, channels).T,
+    output, grad_features, grad_kernel, own_block = step_call(
+        features.reshape(-1, channels),
+        out_grad.reshape(-1, channels),
+        strips,
         kernel.reshape(TAPS, channels, channels),
+        projector,
+        mixers,
     )
-    terms = terms.reshape(NY, NC, NX * TAPS, 64, LANES)
-    grad_kernel, own_block = tree_call(terms, bands, projectors, mixers)
-    shape = (band_rows, band_cols, channels)
     return (output.reshape(shape), grad_features.reshape(shape), grad_kernel, own_block)
 
 

time: 189 us -> 166 us (0.88)
  starting transfers between devices: 33.8 us -> 0 us
  Pallas kernels: 132 us -> 156 us
  waiting for transfers between devices: 12.1 us -> 0 us
    ppermute x14 -> x0, starting transfers between devices: 33.8 us -> none  [the longest x6 13.6 us: ring_gather(): pieces.append(lax.ppermute(v, 'rows', moves))]
    pallas_call x2 -> x1, Pallas kernels: 132 us -> 156 us  [step_call(): pl.pallas_call(step_kernel, in_specs=[pl.BlockSpec(memory_space=pl.ANY)]...]
    ppermute x14 -> x0, waiting for transfers between devices: 12.1 us -> none  [the longest x6 9.65 us: ring_gather(): pieces.append(lax.ppermute(v, 'rows', moves))]
    unnamed x16 -> x4, local copies, waits for them, and re-layouts: 4.81 us -> 6.15 us
  transfers between devices with their start and end apart: 14 -> 0, of which waited for: 3 -> 0; matrix products, arithmetic and copies ran while one was open for 2% -> 0% of each run, Pallas kernels for 4% -> 0%
where the time goes in v2:
time: 166 us; the launch traced here: 165 us
  Pallas kernels  156 us (94%)
  local copies, waits for them, and re-layouts  7.97 us (5%)
    pallas_call x1, Pallas kernels, step_call(): pl.pallas_call(step_kernel, in_specs=[pl.BlockSpec(memory_space=pl.ANY)]...  156 us
    unnamed x4, local copies, waits for them, and re-layouts  6.15 us

profile of v2, /device:TPU:8, one launch (start us, length us, event | category | flops | bytes accessed | tf_op | source)
XLA Modules:
  0.0 165.2 jit_solution(3895701092239579798)
XLA Ops:
  0.6 0.9 fusion
  1.6 0.9 fusion.1
  2.5 0.6 pad_maximum_fusion.strips
  3.1 155.9 %conv_step.1 = (bf16[256,512]{1,0:T(8,128)(2,1)}, bf16[256,512]{1,0:T(8,128)(2,1)}, f32[9,16,64]{2,1,0:T(8,128)}, bf16[16,144]{1,0:T(8,128)(2,1)}) custom-call(bf16[256,512]{1,0:T(8,128)(2,1)} %bitcast.18, bf16[256,512]{1,0:T(8,128)(2,1)} %bitcast.19, bf16[2,16,512]{2,1,0:T(8,128)(2,1)} %pad_maximum_fusion.strips, bf16[9,512,512]{2,1,0:T(8,128)(2,1)} %bitcast.17, ...), custom_call_target="tpu_custom_call" | custom-call | tf_op jit(solution)/shard_map/conv_step/pallas_call | solution.py:385
  159.0 1.7 %copy.25 = bf16[8,32,512]{2,1,0:T(8,128)(2,1)} copy(bf16[8,32,512]{2,1,0:T(8,128)(2,1)} %bitcast.21) | data formatting | bytes 524288
  160.7 1.7 %copy.26 = bf16[8,32,512]{2,1,0:T(8,128)(2,1)} copy(bf16[8,32,512]{2,1,0:T(8,128)(2,1)} %bitcast.20) | data formatting | bytes 524288
  162.4 1.5 copy.27
  163.9 1.3 copy.28
  (4 shorter events, 0.0 us)

commit v3 on v2

--- a/solution.py
+++ b/solution.py
@@ -12,6 +12,7 @@
 RANK = 128
 TAPS = 9
 QUART = 1152
+HALF = 640
 MESH = pl.DeviceIdType.MESH
 F32 = jnp.float32
 BF16 = jnp.bfloat16
@@ -78,9 +79,9 @@
 
 
 def step_kernel(
-    feat, grad, strips, kern, proj, mixers, out, gfeat, gk, sketch,
-    bx, be, pj, gs, edge, line, xsp, ogt, kv, wt, acc,
-    ro, rc, ry, w2, rx, wz, rz, m0, m1, ma, mb, da, db, po, pr, fr, gm, lsem, ssem, rsem,
+    feat, grad, kern, proj, mixers, out, gfeat, gk, sketch,
+    bx, be, pj, gs, strips, cut, edge, line, xsp, ogt, kv, wt, acc,
+    ro, rc, ry, w2, rx, wz, rz, m0, m1, mo, ma, mb, da, db, va, vb, po, pr, fr, gm, lsem, ssem, rsem,
 ):
     row, col = lax.axis_index("rows"), lax.axis_index("cols")
     n_rows, n_cols = NX * NZ, NY * NC
@@ -94,6 +95,9 @@
     y_peers = [at(z, x, lax.rem(y + d, NY), core) for d in range(1, NY)]
     z_peers = [at(lax.rem(z + d, NZ), x, y, core) for d in range(1, NZ)]
     core_peer = at(z, x, y, 1 - core)
+    half = lax.rem(z, 2)
+    mate = z + 1 - 2 * half
+    sum_peers = x_peers + [at(mate, lax.rem(x + d, NX), y, core) for d in range(NX)]
     above, below = lax.rem(row + n_rows - 1, n_rows), lax.rem(row + 1, n_rows)
     before, after = lax.rem(col + n_cols - 1, n_cols), lax.rem(col + 1, n_cols)
     around = [(r, c) for c in (before, after) for r in (above, row, below)]
@@ -110,9 +114,19 @@
     weights = fetch(kern, kv, 3)
 
     barrier = pltpu.get_barrier_semaphore()
-    peers = x_peers + y_peers + z_peers + [core_peer] + around
+    peers = sum_peers + y_peers + z_peers + [core_peer] + around
     for peer in peers:
         pl.semaphore_signal(barrier, inc=1, device_id=peer, device_id_type=MESH)
+    own_band.wait()
+    own_grad.wait()
+    for which, held in enumerate((bx.at[0, 1], gs.at[1])):
+        for h in range(8):
+            at_row = 8 * which + h
+            first = held[32 + h * 32 : 48 + h * 32].astype(F32)
+            last = held[48 + h * 32 : 64 + h * 32].astype(F32)
+            cut[0, at_row : at_row + 1] = first[0:1]
+            cut[1, at_row : at_row + 1] = last[15:16]
+    strips[...] = cut[...].astype(BF16)
     pl.semaphore_wait(barrier, len(peers))
 
     started = []
@@ -132,21 +146,20 @@
 
     halo = []
     for k, r in enumerate((below, row, above)):
-        halo.append(send(strips.at[0], edge.at[1, k], 47 + k, (r, before)))
-        halo.append(send(strips.at[1], edge.at[0, k], 50 + k, (r, after)))
-    halo.append(send(feat.at[224:256], bx.at[0, 1, 0:32], 53, (below, col)))
-    halo.append(send(feat.at[0:32], bx.at[0, 1, 288:320], 54, (above, col)))
-    halo.append(send(grad.at[224:256], gs.at[1, 0:32], 55, (below, col)))
-    halo.append(send(grad.at[0:32], gs.at[1, 288:320], 56, (above, col)))
-    main = [
-        (
-            send(feat, bx.at[d, 1, 32:288], 56 + d, x_peers[d - 1]),
-            send(proj, pj.at[d], 59 + d, x_peers[d - 1]),
+        halo.append(send(strips.at[0], edge.at[1, k], 77 + k, (r, before)))
+        halo.append(send(strips.at[1], edge.at[0, k], 80 + k, (r, after)))
+    halo.append(send(feat.at[224:256], bx.at[0, 1, 0:32], 83, (below, col)))
+    halo.append(send(feat.at[0:32], bx.at[0, 1, 288:320], 84, (above, col)))
+    halo.append(send(grad.at[224:256], gs.at[1, 0:32], 85, (below, col)))
+    halo.append(send(grad.at[0:32], gs.at[1, 288:320], 86, (above, col)))
+    main = {
+        d: (
+            send(feat, bx.at[d, 1, 32:288], 86 + d, x_peers[d - 1]),
+            send(proj, pj.at[d], 89 + d, x_peers[d - 1]),
         )
-        for d in range(1, NX)
-    ]
-    for copy in (own_band, own_grad, own_proj):
-        copy.wait()
+        for d in (2, 1, 3)
+    }
+    own_proj.wait()
     ogt[...] = gs[1, 32:288].astype(F32).T.astype(BF16)
     for copy in halo:
         copy.wait_recv()
@@ -167,14 +180,14 @@
             line[which, side, 1:9] = mid[rows : rows + 8]
             line[which, side, 9:10] = kept(down[rows : rows + 1], bottom)
     be[0] = line[0].astype(BF16)
-    ends = [
-        (
-            send(bx.at[0, 1, 0:32], bx.at[d, 1, 0:32], 62 + d, x_peers[d - 1]),
-            send(bx.at[0, 1, 288:320], bx.at[d, 1, 288:320], 65 + d, x_peers[d - 1]),
-            send(be.at[0], be.at[d], 68 + d, x_peers[d - 1]),
+    ends = {
+        d: (
+            send(bx.at[0, 1, 0:32], bx.at[d, 1, 0:32], 92 + d, x_peers[d - 1]),
+            send(bx.at[0, 1, 288:320], bx.at[d, 1, 288:320], 95 + d, x_peers[d - 1]),
+            send(be.at[0], be.at[d], 98 + d, x_peers[d - 1]),
         )
-        for d in range(1, NX)
-    ]
+        for d in (2, 1, 3)
+    }
     shift_columns(bx, (line[0, 0], line[0, 1]), (0,))
 
     ci = lax.broadcasted_iota(jnp.int32, (CH, CH), 0)
@@ -199,39 +212,53 @@
     core_copy = send(wt.at[:, 1 - core], rc, 0, core_peer)
     shift_columns(gs, (line[1, 0], line[1, 1]), ())
 
-    for d in range(1, NX):
-        for copy in main[d - 1] + ends[d - 1]:
-            copy.wait_recv()
-        edges = be[d].astype(F32)
-        shift_columns(bx, (edges[0], edges[1]), (d,))
-
-    for j in range(NX):
-        slot = lax.rem(x - j + NX, NX)
+    def sketch_band(slot):
+        j = lax.rem(x - slot + NX, NX)
         p = pj[slot]
         for t in range(TAPS):
             a, b = t // 3, t % 3
             part = dot(p, bx[slot, b, a * 32 : a * 32 + 256, :]).astype(BF16)
             for i in range(4):
                 q, lane = (4 * t + i) // 9, (4 * t + i) % 9
-                m0[
-                    j // 2, q, (j % 2) * RANK : (j % 2 + 1) * RANK,
-                    lane * LANES : (lane + 1) * LANES,
-                ] = part[:, i * LANES : (i + 1) * LANES]
+                m0[j, q, :, lane * LANES : (lane + 1) * LANES] = part[
+                    :, i * LANES : (i + 1) * LANES
+                ]
+
+    sketch_band(0)
+    for d in (3, 1, 2):
+        for copy in main[d] + ends[d]:
+            copy.wait_recv()
+        edges = be[d].astype(F32)
+        shift_columns(bx, (edges[0], edges[1]), (d,))
+        sketch_band(d)
+
+    def pair_rows(pair, q):
+        return jnp.concatenate([m0[2 * pair, q], m0[2 * pair + 1, q]], axis=0)
+
     grams = []
     for pair in range(2):
-        gram = dot_t(m0[pair, 0], m0[pair, 0])
-        for q in range(1, 4):
-            gram += dot_t(m0[pair, q], m0[pair, q])
+        gram = jnp.zeros((2 * RANK, 2 * RANK), F32)
+        for q in range(4):
+            stacked = pair_rows(pair, q)
+            gram += dot_t(stacked, stacked)
         grams.append(gram)
     for pair, combiner in enumerate(combiners(grams, mixers[0])):
         for q in range(4):
-            m1[q, pair * RANK : (pair + 1) * RANK, :] = dot(combiner, m0[pair, q]).astype(BF16)
+            m1[q, pair * RANK : (pair + 1) * RANK, :] = dot(combiner, pair_rows(pair, q)).astype(
+                BF16
+            )
 
     gram = dot_t(m1[0], m1[0])
     for q in range(1, 4):
         gram += dot_t(m1[q], m1[q])
     (combiner,) = combiners([gram], mixers[0])
-    ma[0] = dot(combiner, m1[x]).astype(BF16)
+    merged = dot(combiner, m1[x])
+    low, high = merged[:, :HALF], merged[:, QUART - HALF :]
+    ma[0] = jnp.where(half == 0, low, high).astype(BF16)
+    mo[...] = jnp.where(half == 0, high, low).astype(BF16)
+    eye = lax.broadcasted_iota(jnp.int32, (RANK, RANK), 0) == lax.broadcasted_iota(
+        jnp.int32, (RANK, RANK), 1
+    )
 
     def core_stage():
         core_copy.wait_recv()
@@ -315,10 +342,16 @@
         (at(z, x, flip(y, 2), core), lax.div(y, 2), 1),
     ]
     for level, (peer, upper, which) in enumerate(levels):
-        base = 14 + 5 * level
-        slice_copy = send(ma.at[level], mb.at[level], base, peer)
-        da[level] = carried_gram(combiner, gram)
-        gram_copy = send(da.at[level], db.at[level], base + 1, peer)
+        base = 14 + 10 * level
+        slice_copy = send(mo if level == 0 else ma.at[level], mb.at[level], base, peer)
+        within = carried_gram(combiner, gram)
+        straight = jnp.sum(jnp.where(eye, within, 0.0), axis=0, keepdims=True)
+        va[level] = jnp.broadcast_to(straight, (8, RANK))
+        da[level] = jnp.where(eye, 0.0, within).astype(BF16)
+        gram_copies = [
+            send(va.at[level], vb.at[level], base + 1, peer),
+            send(da.at[level], db.at[level], base + 2, peer),
+        ]
         if level == 0:
             y_copies = core_stage()
             forward()
@@ -333,22 +366,28 @@
             upper == 0, mix, jnp.concatenate([mix[:, RANK:], mix[:, :RANK]], axis=1)
         )
         slice_copy.wait_recv()
-        cross = dot_t(ma[level], mb[level]).astype(BF16)
+        shared = 2 * HALF - QUART
+        first = dot_t(ma[level, :, :shared], mb[level, :, :shared])
+        cross = dot_t(ma[level, :, shared:], mb[level, :, shared:])
+        cross = (cross + jnp.where(half == 0, first, 0.0)).astype(BF16)
         po[level] = cross
         cross_copies = [
-            send(po.at[level], pr.at[level, d - 1], base + 1 + d, x_peers[d - 1])
-            for d in range(1, NX)
+            send(po.at[level], pr.at[level, k], base + 3 + k, peer)
+            for k, peer in enumerate(sum_peers)
         ]
-        gram_copy.wait_recv()
-        for copy in cross_copies:
+        for copy in gram_copies + cross_copies:
             copy.wait_recv()
         cross = cross.astype(F32)
-        for d in range(NX - 1):
-            cross += pr[level, d].astype(F32)
-        gm[0:RANK, 0:RANK] = da[level]
+        for k in range(NX - 1):
+            cross += pr[level, k].astype(F32)
+        others = pr[level, NX - 1].astype(F32)
+        for k in range(NX, len(sum_peers)):
+            others += pr[level, k].astype(F32)
+        cross += others.T if level == 0 else others
+        gm[0:RANK, 0:RANK] = jnp.where(eye, va[level, 0:1], da[level].astype(F32))
         gm[0:RANK, RANK:] = cross
         gm[RANK:, 0:RANK] = cross.T
-        gm[RANK:, RANK:] = db[level]
+        gm[RANK:, RANK:] = jnp.where(eye, vb[level, 0:1], db[level].astype(F32))
         gram = gm[...]
         (combiner,) = combiners([gram], mix)
         stacked = jnp.concatenate([ma[level], mb[level]], axis=0)
@@ -358,7 +397,7 @@
     own_rows = pl.ds(pl.multiple_of(col * 16, 16), 16)
     fr[0] = ma[last, own_rows, :]
     final_copies = [
-        send(ma.at[last, own_rows], fr.at[d], 43 + d, x_peers[d - 1]) for d in range(1, NX)
+        send(ma.at[last, own_rows], fr.at[d], 73 + d, x_peers[d - 1]) for d in range(1, NX)
     ]
     for copy in z_copies:
         copy.wait_recv()
@@ -371,20 +410,21 @@
             gk[2 * pair + 1] = total[:, 64:]
     for copy in final_copies:
         copy.wait_recv()
-    k = lax.broadcasted_iota(jnp.int32, (QUART, 144), 0)
-    j = lax.broadcasted_iota(jnp.int32, (QUART, 144), 1)
-    chosen = jnp.where(k == j + lax.rem(row, 8) * 144, 1.0, 0.0).astype(BF16)
+    k = lax.broadcasted_iota(jnp.int32, (HALF, 144), 0)
+    j = lax.broadcasted_iota(jnp.int32, (HALF, 144), 1)
+    skip = lax.rem(row, 8) * 144 - half * (QUART - HALF)
+    chosen = jnp.where(k == j + skip, 1.0, 0.0).astype(BF16)
     held = fr[lax.rem(x - lax.div(z, 2) + NX, NX)]
     sketch[...] = dot(held, chosen).astype(BF16)
     for copy in started:
         copy.wait_send()
 
 
-def step_call(feat, grad, strips, kern, proj, mixers):
+def step_call(feat, grad, kern, proj, mixers):
     vmem = pl.BlockSpec(memory_space=pltpu.VMEM)
     return pl.pallas_call(
         step_kernel,
-        in_specs=[pl.BlockSpec(memory_space=pl.ANY)] * 5 + [vmem],
+        in_specs=[pl.BlockSpec(memory_space=pl.ANY)] * 4 + [vmem],
         out_specs=[vmem] * 4,
         out_shape=[
             jax.ShapeDtypeStruct((256, CH), BF16),
@@ -397,6 +437,8 @@
             pltpu.VMEM((NX, 2, 16, CH), BF16),
             pltpu.VMEM((NX, RANK, 256), BF16),
             pltpu.VMEM((3, 320, CH), BF16),
+            pltpu.VMEM((2, 16, CH), BF16),
+            pltpu.VMEM((2, 16, CH), F32),
             pltpu.VMEM((2, 3, 16, CH), BF16),
             pltpu.VMEM((2, 2, 16, CH), F32),
             pltpu.VMEM((3, 320, CH), BF16),
@@ -411,44 +453,64 @@
             pltpu.VMEM((NX - 1, 9, 64, LANES), BF16),
             pltpu.VMEM((NZ, 5, 16, LANES), BF16),
             pltpu.VMEM((NZ - 1, 5, 16, LANES), BF16),
-            pltpu.VMEM((2, 4, 2 * RANK, QUART), BF16),
+            pltpu.VMEM((4, 4, RANK, QUART), BF16),
             pltpu.VMEM((4, 2 * RANK, QUART), BF16),
-            pltpu.VMEM((7, RANK, QUART), BF16),
-            pltpu.VMEM((6, RANK, QUART), BF16),
-            pltpu.VMEM((6, RANK, RANK), F32),
-            pltpu.VMEM((6, RANK, RANK), F32),
+            pltpu.VMEM((RANK, HALF), BF16),
+            pltpu.VMEM((7, RANK, HALF), BF16),
+            pltpu.VMEM((6, RANK, HALF), BF16),
             pltpu.VMEM((6, RANK, RANK), BF16),
-            pltpu.VMEM((6, 3, RANK, RANK), BF16),
-            pltpu.VMEM((4, 16, QUART), BF16),
+            pltpu.VMEM((6, RANK, RANK), BF16),
+            pltpu.VMEM((6, 8, RANK), F32),
+            pltpu.VMEM((6, 8, RANK), F32),
+            pltpu.VMEM((6, RANK, RANK), BF16),
+            pltpu.VMEM((6, 7, RANK, RANK), BF16),
+            pltpu.VMEM((4, 16, HALF), BF16),
             pltpu.VMEM((2 * RANK, 2 * RANK), F32),
             pltpu.SemaphoreType.DMA((4,)),
-            pltpu.SemaphoreType.DMA((72,)),
-            pltpu.SemaphoreType.DMA((72,)),
+            pltpu.SemaphoreType.DMA((102,)),
+            pltpu.SemaphoreType.DMA((102,)),
         ],
         compiler_params=pltpu.CompilerParams(
             collective_id=0, has_side_effects=True, vmem_limit_bytes=56 << 20
         ),
         name="conv_step",
-    )(feat, grad, strips, kern, proj, mixers)
+    )(feat, grad, kern, proj, mixers)
+
+
+def settle_kernel(*refs):
+    sem = refs[-1]
+    copies = [
+        pltpu.make_async_copy(refs[i], refs[i + 4], sem.at[i]) for i in range(4)
+    ]
+    for copy in copies:
+        copy.start()
+    for copy in copies:
+        copy.wait()
+
+
+def settle(results):
+    anywhere = [pl.BlockSpec(memory_space=pl.ANY)] * 4
+    return pl.pallas_call(
+        settle_kernel,
+        in_specs=anywhere,
+        out_specs=anywhere,
+        out_shape=[jax.ShapeDtypeStruct(r.shape, r.dtype) for r in results],
+        scratch_shapes=[pltpu.SemaphoreType.DMA((4,))],
+        name="results",
+    )(*results)
 
 
 def body(features, kernel, out_grad, projector, mixers):
     shape = features.shape
     channels = shape[2]
-    strips = jnp.stack(
-        [
-            jnp.concatenate([features[:, w], out_grad[:, w]], axis=0)
-            for w in (0, shape[1] - 1)
-        ]
-    )
-    output, grad_features, grad_kernel, own_block = step_call(
+    results = step_call(
         features.reshape(-1, channels),
         out_grad.reshape(-1, channels),
-        strips,
         kernel.reshape(TAPS, channels, channels),
         projector,
         mixers,
     )
+    output, grad_features, grad_kernel, own_block = settle(results)
     return (output.reshape(shape), grad_features.reshape(shape), grad_kernel, own_block)
 
 

time: 166 us -> 155 us (0.934)
  local copies, waits for them, and re-layouts: 7.97 us -> 0 us
  Pallas kernels: 156 us -> 154 us
    pallas_call x1, Pallas kernels: 156 us -> 134 us  [step_call(): pl.pallas_call(step_kernel, in_specs=[pl.BlockSpec(memory_space=pl.ANY)]...]
    pallas_call x0 -> x1, Pallas kernels: none -> 19.5 us  [settle(): pl.pallas_call(settle_kernel, in_specs=anywhere, out_specs=anywhere, out_...]
    unnamed x4 -> x0, local copies, waits for them, and re-layouts: 6.15 us -> none
    slice x2 -> x0, local copies, waits for them, and re-layouts: 1.81 us -> none  [the longest x1 0.9 us: body(): features[:, w]]
where the time goes in v3:
time: 155 us
  Pallas kernels  154 us (99%)
    pallas_call x1, Pallas kernels, step_call(): pl.pallas_call(step_kernel, in_specs=[pl.BlockSpec(memory_space=pl.ANY)]...  134 us
    pallas_call x1, Pallas kernels, settle(): pl.pallas_call(settle_kernel, in_specs=anywhere, out_specs=anywhere, out_...  19.5 us

profile of v3, /device:TPU:8, one launch (start us, length us, event | category | flops | bytes accessed | tf_op | source)
XLA Modules:
  0.0 154.7 jit_solution(14329966063679151514)
XLA Ops:
  0.6 134.4 %conv_step.1 = (bf16[256,512]{1,0:T(8,128)(2,1)}, bf16[256,512]{1,0:T(8,128)(2,1)}, f32[9,16,64]{2,1,0:T(8,128)}, bf16[16,144]{1,0:T(8,128)(2,1)}) custom-call(bf16[256,512]{1,0:T(8,128)(2,1)} %bitcast.6, bf16[256,512]{1,0:T(8,128)(2,1)} %bitcast.7, bf16[9,512,512]{2,1,0:T(8,128)(2,1)} %bitcast.5, bf16[128,256]{1,0:T(8,128)(2,1)} %proj.1, ...), custom_call_target="tpu_custom_call" | custom-call | tf_op jit(solution)/shard_map/conv_step/pallas_call | solution.py:425
  135.0 19.5 %results.1 = (bf16[256,512]{1,0:T(8,128)(2,1)}, bf16[256,512]{1,0:T(8,128)(2,1)}, f32[9,16,64]{2,1,0:T(8,128)}, bf16[16,144]{1,0:T(8,128)(2,1)}) custom-call(bf16[256,512]{1,0:T(8,128)(2,1)} %get-tuple-element.12.refs_0_, bf16[256,512]{1,0:T(8,128)(2,1)} %get-tuple-element.13.refs_1_, f32[9,16,64]{2,1,0:T(8,128)} %get-tuple-element.14.refs_2_, ...), custom_call_target="tpu_custom_call" | custom-call | tf_op jit(solution)/shard_map/results/pallas_call | solution.py:493

commit v4 on v3

--- a/solution.py
+++ b/solution.py
@@ -478,24 +478,17 @@
 
 
 def settle_kernel(*refs):
-    sem = refs[-1]
-    copies = [
-        pltpu.make_async_copy(refs[i], refs[i + 4], sem.at[i]) for i in range(4)
-    ]
-    for copy in copies:
-        copy.start()
-    for copy in copies:
-        copy.wait()
+    for held, result in zip(refs[:4], refs[4:]):
+        result[...] = held[...]
 
 
 def settle(results):
-    anywhere = [pl.BlockSpec(memory_space=pl.ANY)] * 4
+    vmem = [pl.BlockSpec(memory_space=pltpu.VMEM)] * 4
     return pl.pallas_call(
         settle_kernel,
-        in_specs=anywhere,
-        out_specs=anywhere,
+        in_specs=vmem,
+        out_specs=vmem,
         out_shape=[jax.ShapeDtypeStruct(r.shape, r.dtype) for r in results],
-        scratch_shapes=[pltpu.SemaphoreType.DMA((4,))],
         name="results",
     )(*results)
 

time: 155 us -> 137 us (0.88)
  Pallas kernels: 154 us -> 136 us
    pallas_call x1, Pallas kernels: 19.5 us -> 1.87 us  [settle(): pl.pallas_call(settle_kernel, in_specs=vmem, out_specs=vmem, out_shape=[j...]
where the time goes in v4:
time: 137 us
  Pallas kernels  136 us (99%)
    pallas_call x1, Pallas kernels, step_call(): pl.pallas_call(step_kernel, in_specs=[pl.BlockSpec(memory_space=pl.ANY)]...  134 us

profile of v4, /device:TPU:8, one launch (start us, length us, event | category | flops | bytes accessed | tf_op | source)
XLA Modules:
  0.0 136.9 jit_solution(6983773750548991749)
XLA Ops:
  0.6 134.4 %conv_step.1 = (bf16[256,512]{1,0:T(8,128)(2,1)}, bf16[256,512]{1,0:T(8,128)(2,1)}, f32[9,16,64]{2,1,0:T(8,128)}, bf16[16,144]{1,0:T(8,128)(2,1)}) custom-call(bf16[256,512]{1,0:T(8,128)(2,1)} %bitcast.6, bf16[256,512]{1,0:T(8,128)(2,1)} %bitcast.7, bf16[9,512,512]{2,1,0:T(8,128)(2,1)} %bitcast.5, bf16[128,256]{1,0:T(8,128)(2,1)} %proj.1, ...), custom_call_target="tpu_custom_call" | custom-call | tf_op jit(solution)/shard_map/conv_step/pallas_call | solution.py:425
  135.0 1.9 %results.1 = (bf16[256,512]{1,0:T(8,128)(2,1)}, bf16[256,512]{1,0:T(8,128)(2,1)}, f32[9,16,64]{2,1,0:T(8,128)}, bf16[16,144]{1,0:T(8,128)(2,1)}) custom-call(bf16[256,512]{1,0:T(8,128)(2,1)} %get-tuple-element.12.refs_0_, bf16[256,512]{1,0:T(8,128)(2,1)} %get-tuple-element.13.refs_1_, f32[9,16,64]{2,1,0:T(8,128)} %get-tuple-element.14.refs_2_, ...), custom_call_target="tpu_custom_call" | custom-call | tf_op jit(solution)/shard_map/results/pallas_call | solution.py:487

commit v5 on v4

--- a/solution.py
+++ b/solution.py
@@ -13,6 +13,7 @@
 TAPS = 9
 QUART = 1152
 HALF = 640
+FAR_FIRST = (4, 3, 5, 6, 1, 0, 2)
 MESH = pl.DeviceIdType.MESH
 F32 = jnp.float32
 BF16 = jnp.bfloat16
@@ -38,25 +39,23 @@
     eye = jnp.where(i == j, 1.0, 0.0)
     trace = jnp.sum(gram * eye, keepdims=True)
     spread = gram / (trace + 1e-06) - eye * (1.0 / size)
-    return spread / (jnp.sqrt(jnp.sum(spread * spread, keepdims=True)) + 1e-06)
-
-
-def combiners(grams, mix):
-    spreads = [start_spread(gram) for gram in grams]
-    for sweep in range(NS_STEPS - 1):
-        rounded = [s.astype(BF16) for s in spreads]
-        squares = [dot(r, r).astype(BF16) for r in rounded]
-        spreads = [
-            1.5 * s - 0.5 * dot(r, q) for s, r, q in zip(spreads, rounded, squares)
-        ]
-    parts = [split(s) for s in spreads]
-    squares = [dot(high, high).astype(BF16) for high, low in parts]
-    mixed = [dot(mix, high) + dot(mix, low) for high, low in parts]
-    wide = mix.astype(F32)
-    return [
-        (0.5 * wide + 0.75 * m - 0.25 * dot(m.astype(BF16), q)).astype(BF16)
-        for m, q in zip(mixed, squares)
-    ]
+    return spread, jnp.sum(spread * spread, keepdims=True)
+
+
+def combined(spread, squared_norm, mix):
+    scale = 1.0 / (jnp.sqrt(squared_norm) + 1e-06)
+    rounded = spread.astype(BF16)
+    cubed = dot(rounded, dot(rounded, rounded).astype(BF16))
+    spread = (1.5 * scale) * spread - (0.5 * scale * scale * scale) * cubed
+    for sweep in range(NS_STEPS - 2):
+        rounded = spread.astype(BF16)
+        square = dot(rounded, rounded).astype(BF16)
+        spread = 1.5 * spread - 0.5 * dot(rounded, square)
+    high, low = split(spread)
+    square = dot(high, high).astype(BF16)
+    mixed = dot(mix, high) + dot(mix, low)
+    wide = 0.5 * mix.astype(F32) + 0.75 * mixed
+    return (wide - 0.25 * dot(mixed.astype(BF16), square)).astype(BF16)
 
 
 def carried_gram(combiner, gram):
@@ -81,7 +80,7 @@
 def step_kernel(
     feat, grad, kern, proj, mixers, out, gfeat, gk, sketch,
     bx, be, pj, gs, strips, cut, edge, line, xsp, ogt, kv, wt, acc,
-    ro, rc, ry, w2, rx, wz, rz, m0, m1, mo, ma, mb, da, db, va, vb, po, pr, fr, gm, lsem, ssem, rsem,
+    ro, rc, ry, w2, rx, wz, rz, m0, m1, mo, ma, mb, da, db, va, vb, po, pr, fr, gm, ym, lsem, ssem, rsem,
 ):
     row, col = lax.axis_index("rows"), lax.axis_index("cols")
     n_rows, n_cols = NX * NZ, NY * NC
@@ -224,35 +223,39 @@
                     :, i * LANES : (i + 1) * LANES
                 ]
 
-    sketch_band(0)
-    for d in (3, 1, 2):
+    def receive_band(d):
         for copy in main[d] + ends[d]:
             copy.wait_recv()
         edges = be[d].astype(F32)
         shift_columns(bx, (edges[0], edges[1]), (d,))
         sketch_band(d)
 
-    def pair_rows(pair, q):
-        return jnp.concatenate([m0[2 * pair, q], m0[2 * pair + 1, q]], axis=0)
-
-    grams = []
-    for pair in range(2):
+    def merge_pair(pair):
         gram = jnp.zeros((2 * RANK, 2 * RANK), F32)
         for q in range(4):
-            stacked = pair_rows(pair, q)
+            stacked = jnp.concatenate([m0[2 * pair, q], m0[2 * pair + 1, q]], axis=0)
             gram += dot_t(stacked, stacked)
-        grams.append(gram)
-    for pair, combiner in enumerate(combiners(grams, mixers[0])):
+        combiner = combined(*start_spread(gram), mixers[0])
         for q in range(4):
-            m1[q, pair * RANK : (pair + 1) * RANK, :] = dot(combiner, pair_rows(pair, q)).astype(
-                BF16
-            )
-
-    gram = dot_t(m1[0], m1[0])
-    for q in range(1, 4):
-        gram += dot_t(m1[q], m1[q])
-    (combiner,) = combiners([gram], mixers[0])
-    merged = dot(combiner, m1[x])
+            stacked = jnp.concatenate([m0[2 * pair, q], m0[2 * pair + 1, q]], axis=0)
+            m1[pair, q] = dot(combiner, stacked).astype(BF16)
+
+    sketch_band(0)
+    receive_band(3)
+    receive_band(1)
+    merge_pair(lax.div(x, 2))
+    receive_band(2)
+    merge_pair(1 - lax.div(x, 2))
+
+    def quarter(q):
+        return jnp.concatenate([m1[0, q], m1[1, q]], axis=0)
+
+    gram = jnp.zeros((2 * RANK, 2 * RANK), F32)
+    for q in range(4):
+        stacked = quarter(q)
+        gram += dot_t(stacked, stacked)
+    combiner = combined(*start_spread(gram), mixers[0])
+    merged = dot(combiner, quarter(x))
     low, high = merged[:, :HALF], merged[:, QUART - HALF :]
     ma[0] = jnp.where(half == 0, low, high).astype(BF16)
     mo[...] = jnp.where(half == 0, high, low).astype(BF16)
@@ -344,7 +347,7 @@
     for level, (peer, upper, which) in enumerate(levels):
         base = 14 + 10 * level
         slice_copy = send(mo if level == 0 else ma.at[level], mb.at[level], base, peer)
-        within = carried_gram(combiner, gram)
+        within = carried_gram(combiner, gram if level == 0 else gm[...])
         straight = jnp.sum(jnp.where(eye, within, 0.0), axis=0, keepdims=True)
         va[level] = jnp.broadcast_to(straight, (8, RANK))
         da[level] = jnp.where(eye, 0.0, within).astype(BF16)
@@ -354,10 +357,10 @@
         ]
         if level == 0:
             y_copies = core_stage()
+        if level == 1:
             forward()
-        if level == 1:
+        if level == 2:
             backward()
-        if level == 2:
             x_copies = y_stage()
         if level == 4:
             z_copies = x_stage()
@@ -373,9 +376,20 @@
         po[level] = cross
         cross_copies = [
             send(po.at[level], pr.at[level, k], base + 3 + k, peer)
-            for k, peer in enumerate(sum_peers)
+            for k, peer in sorted(enumerate(sum_peers), key=lambda item: FAR_FIRST[item[0]])
         ]
-        for copy in gram_copies + cross_copies:
+        for copy in gram_copies:
+            copy.wait_recv()
+        trace = jnp.sum(va[level, 0:1] + vb[level, 0:1], keepdims=True) + 1e-06
+        squared_norm = jnp.zeros((1, 1), F32)
+        for k, (straight, rest) in enumerate(((va, da), (vb, db))):
+            part = slice(k * RANK, (k + 1) * RANK)
+            within = jnp.where(eye, straight[level, 0:1], rest[level].astype(F32))
+            gm[part, part] = within
+            within = within / trace - jnp.where(eye, 0.5 / RANK, 0.0)
+            ym[part, part] = within
+            squared_norm += jnp.sum(within * within, keepdims=True)
+        for copy in cross_copies:
             copy.wait_recv()
         cross = cross.astype(F32)
         for k in range(NX - 1):
@@ -384,14 +398,15 @@
         for k in range(NX, len(sum_peers)):
             others += pr[level, k].astype(F32)
         cross += others.T if level == 0 else others
-        gm[0:RANK, 0:RANK] = jnp.where(eye, va[level, 0:1], da[level].astype(F32))
+        scaled = cross / trace
+        ym[0:RANK, RANK:] = scaled
+        ym[RANK:, 0:RANK] = scaled.T
+        squared_norm += 2.0 * jnp.sum(scaled * scaled, keepdims=True)
+        combiner = combined(ym[...], squared_norm, mix)
+        stacked = jnp.concatenate([ma[level], mb[level]], axis=0)
+        ma[level + 1] = dot(combiner, stacked).astype(BF16)
         gm[0:RANK, RANK:] = cross
         gm[RANK:, 0:RANK] = cross.T
-        gm[RANK:, RANK:] = jnp.where(eye, vb[level, 0:1], db[level].astype(F32))
-        gram = gm[...]
-        (combiner,) = combiners([gram], mix)
-        stacked = jnp.concatenate([ma[level], mb[level]], axis=0)
-        ma[level + 1] = dot(combiner, stacked).astype(BF16)
 
     last = len(levels)
     own_rows = pl.ds(pl.multiple_of(col * 16, 16), 16)
@@ -427,10 +442,10 @@
         in_specs=[pl.BlockSpec(memory_space=pl.ANY)] * 4 + [vmem],
         out_specs=[vmem] * 4,
         out_shape=[
-            jax.ShapeDtypeStruct((256, CH), BF16),
-            jax.ShapeDtypeStruct((256, CH), BF16),
-            jax.ShapeDtypeStruct((TAPS, 16, 64), F32),
-            jax.ShapeDtypeStruct((16, 144), BF16),
+            pltpu.VMEM((256, CH), BF16),
+            pltpu.VMEM((256, CH), BF16),
+            pltpu.VMEM((TAPS, 16, 64), F32),
+            pltpu.VMEM((16, 144), BF16),
         ],
         scratch_shapes=[
             pltpu.VMEM((NX, 3, 320, CH), BF16),
@@ -454,7 +469,7 @@
             pltpu.VMEM((NZ, 5, 16, LANES), BF16),
             pltpu.VMEM((NZ - 1, 5, 16, LANES), BF16),
             pltpu.VMEM((4, 4, RANK, QUART), BF16),
-            pltpu.VMEM((4, 2 * RANK, QUART), BF16),
+            pltpu.VMEM((2, 4, RANK, QUART), BF16),
             pltpu.VMEM((RANK, HALF), BF16),
             pltpu.VMEM((7, RANK, HALF), BF16),
             pltpu.VMEM((6, RANK, HALF), BF16),
@@ -466,6 +481,7 @@
             pltpu.VMEM((6, 7, RANK, RANK), BF16),
             pltpu.VMEM((4, 16, HALF), BF16),
             pltpu.VMEM((2 * RANK, 2 * RANK), F32),
+            pltpu.VMEM((2 * RANK, 2 * RANK), F32),
             pltpu.SemaphoreType.DMA((4,)),
             pltpu.SemaphoreType.DMA((102,)),
             pltpu.SemaphoreType.DMA((102,)),
@@ -490,7 +506,7 @@
         out_specs=vmem,
         out_shape=[jax.ShapeDtypeStruct(r.shape, r.dtype) for r in results],
         name="results",
-    )(*results)
+    )(*[pltpu.with_memory_space_constraint(r, pltpu.VMEM) for r in results])
 
 
 def body(features, kernel, out_grad, projector, mixers):

time: 137 us -> 133 us (0.971)
  Pallas kernels: 136 us -> 132 us
    pallas_call x1, Pallas kernels: 134 us -> 131 us  [step_call(): pl.pallas_call(step_kernel, in_specs=[pl.BlockSpec(memory_space=pl.ANY)]...]
where the time goes in v5:
time: 133 us; the launch traced here: 132 us
  Pallas kernels  132 us (99%)
    pallas_call x1, Pallas kernels, step_call(): pl.pallas_call(step_kernel, in_specs=[pl.BlockSpec(memory_space=pl.ANY)]...  131 us

profile of v5, /device:TPU:8, one launch (start us, length us, event | category | flops | bytes accessed | tf_op | source)
XLA Modules:
  0.0 132.3 jit_solution(18395625284362783231)
XLA Ops:
  0.6 130.8 %conv_step.1 = (bf16[256,512]{1,0:T(8,128)(2,1)S(1)}, bf16[256,512]{1,0:T(8,128)(2,1)S(1)}, f32[9,16,64]{2,1,0:T(8,128)S(1)}, bf16[16,144]{1,0:T(8,128)(2,1)S(1)}) custom-call(bf16[256,512]{1,0:T(8,128)(2,1)} %bitcast.6, bf16[256,512]{1,0:T(8,128)(2,1)} %bitcast.7, bf16[9,512,512]{2,1,0:T(8,128)(2,1)} %bitcast.5, bf16[128,256]{1,0:T(8,128)(2,1)} %proj.1, ...), custom_call_target="tpu_custom_call" | custom-call | tf_op jit(solution)/shard_map/conv_step/pallas_call | solution.py:440
  131.5 0.8 results.1

commit v6 on v5

--- a/solution.py
+++ b/solution.py
@@ -42,20 +42,27 @@
     return spread, jnp.sum(spread * spread, keepdims=True)
 
 
-def combined(spread, squared_norm, mix):
-    scale = 1.0 / (jnp.sqrt(squared_norm) + 1e-06)
-    rounded = spread.astype(BF16)
-    cubed = dot(rounded, dot(rounded, rounded).astype(BF16))
-    spread = (1.5 * scale) * spread - (0.5 * scale * scale * scale) * cubed
+def combined(starts, mix):
+    spreads = []
+    for spread, squared_norm in starts:
+        scale = 1.0 / (jnp.sqrt(squared_norm) + 1e-06)
+        rounded = spread.astype(BF16)
+        cubed = dot(rounded, dot(rounded, rounded).astype(BF16))
+        spreads.append(
+            (1.5 * scale) * spread - (0.5 * scale * scale * scale) * cubed
+        )
     for sweep in range(NS_STEPS - 2):
-        rounded = spread.astype(BF16)
-        square = dot(rounded, rounded).astype(BF16)
-        spread = 1.5 * spread - 0.5 * dot(rounded, square)
-    high, low = split(spread)
-    square = dot(high, high).astype(BF16)
-    mixed = dot(mix, high) + dot(mix, low)
-    wide = 0.5 * mix.astype(F32) + 0.75 * mixed
-    return (wide - 0.25 * dot(mixed.astype(BF16), square)).astype(BF16)
+        rounded = [s.astype(BF16) for s in spreads]
+        squares = [dot(r, r).astype(BF16) for r in rounded]
+        spreads = [1.5 * s - 0.5 * dot(r, q) for s, r, q in zip(spreads, rounded, squares)]
+    parts = [split(s) for s in spreads]
+    squares = [dot(high, high).astype(BF16) for high, low in parts]
+    mixed = [dot(mix, high) + dot(mix, low) for high, low in parts]
+    wide = 0.5 * mix.astype(F32)
+    return [
+        (wide + 0.75 * m - 0.25 * dot(m.astype(BF16), q)).astype(BF16)
+        for m, q in zip(mixed, squares)
+    ]
 
 
 def carried_gram(combiner, gram):
@@ -230,22 +237,23 @@
         shift_columns(bx, (edges[0], edges[1]), (d,))
         sketch_band(d)
 
-    def merge_pair(pair):
+    sketch_band(0)
+    for d in (3, 1, 2):
+        receive_band(d)
+
+    def pair_rows(pair, q):
+        return jnp.concatenate([m0[2 * pair, q], m0[2 * pair + 1, q]], axis=0)
+
+    starts = []
+    for pair in range(2):
         gram = jnp.zeros((2 * RANK, 2 * RANK), F32)
         for q in range(4):
-            stacked = jnp.concatenate([m0[2 * pair, q], m0[2 * pair + 1, q]], axis=0)
+            stacked = pair_rows(pair, q)
             gram += dot_t(stacked, stacked)
-        combiner = combined(*start_spread(gram), mixers[0])
+        starts.append(start_spread(gram))
+    for pair, combiner in enumerate(combined(starts, mixers[0])):
         for q in range(4):
-            stacked = jnp.concatenate([m0[2 * pair, q], m0[2 * pair + 1, q]], axis=0)
-            m1[pair, q] = dot(combiner, stacked).astype(BF16)
-
-    sketch_band(0)
-    receive_band(3)
-    receive_band(1)
-    merge_pair(lax.div(x, 2))
-    receive_band(2)
-    merge_pair(1 - lax.div(x, 2))
+            m1[pair, q] = dot(combiner, pair_rows(pair, q)).astype(BF16)
 
     def quarter(q):
         return jnp.concatenate([m1[0, q], m1[1, q]], axis=0)
@@ -254,7 +262,7 @@
     for q in range(4):
         stacked = quarter(q)
         gram += dot_t(stacked, stacked)
-    combiner = combined(*start_spread(gram), mixers[0])
+    (combiner,) = combined([start_spread(gram)], mixers[0])
     merged = dot(combiner, quarter(x))
     low, high = merged[:, :HALF], merged[:, QUART - HALF :]
     ma[0] = jnp.where(half == 0, low, high).astype(BF16)
@@ -402,7 +410,7 @@
         ym[0:RANK, RANK:] = scaled
         ym[RANK:, 0:RANK] = scaled.T
         squared_norm += 2.0 * jnp.sum(scaled * scaled, keepdims=True)
-        combiner = combined(ym[...], squared_norm, mix)
+        (combiner,) = combined([(ym[...], squared_norm)], mix)
         stacked = jnp.concatenate([ma[level], mb[level]], axis=0)
         ma[level + 1] = dot(combiner, stacked).astype(BF16)
         gm[0:RANK, RANK:] = cross

time: 133 us -> 129 us (0.970)
  Pallas kernels: 132 us -> 127 us
    pallas_call x1, Pallas kernels: 131 us -> 127 us  [step_call(): pl.pallas_call(step_kernel, in_specs=[pl.BlockSpec(memory_space=pl.ANY)]...]
where the time goes in v6:
time: 129 us; the launch traced here: 128 us
  Pallas kernels  127 us (98%)
    pallas_call x1, Pallas kernels, step_call(): pl.pallas_call(step_kernel, in_specs=[pl.BlockSpec(memory_space=pl.ANY)]...  127 us

profile of v6, /device:TPU:8, one launch (start us, length us, event | category | flops | bytes accessed | tf_op | source)
XLA Modules:
  0.0 128.0 jit_solution(1513251571403589192)
XLA Ops:
  0.6 126.5 %conv_step.1 = (bf16[256,512]{1,0:T(8,128)(2,1)S(1)}, bf16[256,512]{1,0:T(8,128)(2,1)S(1)}, f32[9,16,64]{2,1,0:T(8,128)S(1)}, bf16[16,144]{1,0:T(8,128)(2,1)S(1)}) custom-call(bf16[256,512]{1,0:T(8,128)(2,1)} %bitcast.6, bf16[256,512]{1,0:T(8,128)(2,1)} %bitcast.7, bf16[9,512,512]{2,1,0:T(8,128)(2,1)} %bitcast.5, bf16[128,256]{1,0:T(8,128)(2,1)} %proj.1, ...), custom_call_target="tpu_custom_call" | custom-call | tf_op jit(solution)/shard_map/conv_step/pallas_call | solution.py:448
  127.2 0.8 results.1
